TPU v7x, 1024 devices: a whole 4x8x16 slice. The times are simulated.
1024 devices in a mesh: height: 128 (over x, z, core), cols: 8 (over y).
Axes of the slice: x: 4, y: 8, z: 16, core: 2. Of those that a mesh axis runs over, the one named last changes fastest.
Arguments:
- positions: float32 [3, 256, 64, 128], P(None, 'height', 'cols'), may hold values from -0.5 to 0.5
- velocities: float32 [3, 256, 64, 128], P(None, 'height', 'cols'), may hold values from -3 to 3
- contacts: int32 [9, 256, 64], P(None, 'height', 'cols'), may hold values 0 or 1
- exit_flags: int32 [256, 64], P('height', 'cols'), may hold values from 0 to 1, as said below
- inlet_slots: int32 [128, 64], P('height', 'cols'), may hold values from 0 to 7, as said below
- cell_blocks: int32 [256, 64], P('height', 'cols'), may hold values from 0 to 511
- cell_slots: int32 [256, 64, 128], P('height', 'cols'), may hold values from 0 to 127
- gas_source: float32 [256, 512, 512], P('height', 'cols'), may hold values from -12 to 12
- diagonal: float32 [256, 512, 512], P('height', 'cols'), may hold values from 0.25 to 2
Outputs:
- positions_out: float32 [3, 256, 64, 128], P(None, 'height', 'cols')
- velocities_out: float32 [3, 256, 64, 128], P(None, 'height', 'cols')
- pressure: float32 [256, 512, 512], P('height', 'cols')
- residual: float32 [256, 512, 512], P('height', 'cols')
Inputs may be any that keep to these rules, and one draw needn't show every extreme that they name: `exit_flags`: only the top tile row of each device's 2 tile rows holds ones; at most 8 ones on one device, exactly 8 on some device. `inlet_slots`: each device's 8 entries are a permutation of 0 to 7.
All inputs are finite; a program needn't handle non-finite values. No bound on the sum of `contacts` on one device may be relied on, other than what follows from the above.
Results may differ from a plain program's by a relative error of at most 0.0003.
Values sent between devices are 32-bit elements; how exact they have to be, the bound alone decides.
A program may use at most 32 MiB of HBM per device.

v0:
```python
import jax
import jax.numpy as jnp
from jax import lax
from jax.sharding import PartitionSpec as P

ITERS = 2


spring = 0.05
cutoff_sq = 1.44
damping = 0.5
step_dt = 0.05
gravity = 1.0
deposit_gain = 2.0
highest = lax.Precision.HIGHEST


def padded_2(block, sides, width):
    for axis, dim in sides:
        count = lax.axis_size(axis)
        forward = [(i, i + 1) for i in range(count - 1)]
        backward = [(target, source) for source, target in forward]
        low = lax.ppermute(
            lax.slice_in_dim(block, block.shape[dim] - width, None, axis=dim), axis, forward
        )
        high = lax.ppermute(lax.slice_in_dim(block, 0, width, axis=dim), axis, backward)
        block = jnp.concatenate([low, block, high], axis=dim)
    return block


def shifted(value, axis, steps):
    count = lax.axis_size(axis)
    pairs = [(source, (source + steps) % count) for source in range(count)]
    return lax.ppermute(value, axis, pairs)


def row_forces(window, flags):
    width = flags.shape[1]
    centre = window[:, 1, 1 : width + 1, :]
    places = centre[0:3]
    moving = places - damping * centre[3:6]
    own_sq = jnp.sum(places * places, axis=0)
    total = jnp.zeros(places.shape, jnp.float32)
    for row_step in range(3):
        for col_step in range(3):
            other = window[:, row_step, col_step : col_step + width, :]
            offset = jnp.array([col_step - 1.0, 0.0, row_step - 1.0], jnp.float32)[:, None, None]
            other_places = other[0:3] + offset
            cross = jnp.einsum("cip,ciq->ipq", places, other_places, precision=highest)
            other_sq = jnp.sum(other_places * other_places, axis=0)
            dist_sq = own_sq[:, :, None] + other_sq[:, None, :] - 2.0 * cross
            active = flags[row_step * 3 + col_step].astype(jnp.float32)
            weight = spring * jnp.maximum(1.0 - dist_sq / cutoff_sq, 0.0) * active[:, None, None]
            pulled = jnp.einsum(
                "ipq,ciq->cip", weight, other_places - damping * other[3:6], precision=highest
            )
            total = total + moving * jnp.sum(weight, axis=2)[None] - pulled
    return total


def tile_forces(extended, flags):
    count = flags.shape[1]

    def one_row(index):
        window = lax.dynamic_slice_in_dim(extended, index, 3, 1)
        row_flags = lax.dynamic_slice_in_dim(flags, index, 1, 1)[:, 0]
        return row_forces(window, row_flags)

    stacked = lax.map(one_row, jnp.arange(count, dtype=jnp.int32))
    return jnp.transpose(stacked, (1, 0, 2, 3))


def advance(state, forces):
    upward = jnp.array([0.0, 0.0, 1.0], jnp.float32)[:, None, None, None]
    speeds = state[3:6] + step_dt * forces - step_dt * gravity * upward
    places = state[0:3] + step_dt * speeds
    return jnp.concatenate([places, speeds], axis=0)


def operate(field, diagonal):
    padded = padded_2(field, (("height", 0), ("cols", 1)), 1)
    padded = jnp.pad(padded, ((0, 0), (0, 0), (1, 1)))
    beside_all = padded[2:, 1:-1, 1:-1] + padded[:-2, 1:-1, 1:-1]
    beside_all = beside_all + padded[1:-1, 2:, 1:-1] + padded[1:-1, :-2, 1:-1]
    beside_all = beside_all + padded[1:-1, 1:-1, 2:] + padded[1:-1, 1:-1, :-2]
    return (6.0 + diagonal) * field - beside_all


def global_dot(left, right):
    return lax.psum(jnp.sum(left * right), ("height", "cols"))


def on_device(
    positions,
    velocities,
    contacts,
    exit_flags,
    inlet_slots,
    cell_blocks,
    cell_slots,
    gas_source,
    diagonal,
):
    state = jnp.concatenate([positions, velocities], axis=0)
    tile_rows = state.shape[1]
    tile_cols = state.shape[2]
    parts = state.shape[3]
    for repeat in range(2):
        extended = padded_2(state, (("height", 1), ("cols", 2)), 1)
        state = advance(state, tile_forces(extended, contacts))
    settled = state
    flat_flags = exit_flags.reshape(-1)
    tiles = settled.reshape(6, tile_rows * tile_cols, parts)
    ranks = jnp.cumsum(flat_flags) - 1
    buffer_ids = jnp.arange(tile_cols, dtype=jnp.int32)
    picker = ((ranks[None, :] == buffer_ids[:, None]) & (flat_flags[None, :] > 0)).astype(
        jnp.float32
    )
    outgoing = jnp.einsum("kt,ctp->ckp", picker, tiles, precision=highest)
    kept = tiles * (1 - flat_flags).astype(jnp.float32)[None, :, None]
    arrived = shifted(outgoing, "height", 1)
    placing = (inlet_slots[0][None, :] == buffer_ids[:, None]).astype(jnp.float32)
    bottom = jnp.einsum("jk,ckp->cjp", placing, arrived, precision=highest)
    tiles = jnp.concatenate([bottom, kept[:, tile_cols:, :]], axis=1)
    state = tiles.reshape(6, tile_rows, tile_cols, parts)
    lifting = deposit_gain * settled[5].reshape(tile_rows * tile_cols, parts)
    slot_table = (
        cell_slots.reshape(tile_rows * tile_cols, parts)[:, :, None]
        == jnp.arange(parts, dtype=jnp.int32)[None, None, :]
    ).astype(jnp.float32)
    per_tile = jnp.einsum("tp,tpc->tc", lifting, slot_table, precision=highest)
    blocks = gas_source.size // parts
    block_table = (
        jnp.arange(blocks, dtype=jnp.int32)[:, None] == cell_blocks.reshape(-1)[None, :]
    ).astype(jnp.float32)
    deposited = jnp.dot(block_table, per_tile, precision=highest).reshape(gas_source.shape)
    right_side = gas_source - deposited
    scaling = 1.0 / (6.0 + diagonal)
    solution = jnp.zeros_like(right_side)
    residual = right_side
    precond = residual * scaling
    weighted = global_dot(residual, precond)
    direction = precond
    for step in range(ITERS):
        image = operate(direction, diagonal)
        alpha = weighted / global_dot(direction, image)
        solution = solution + alpha * direction
        residual = residual - alpha * image
        if step + 1 < ITERS:
            precond = residual * scaling
            renewed = global_dot(residual, precond)
            direction = precond + renewed / weighted * direction
            weighted = renewed
    return (state[0:3], state[3:6], solution, residual)


def solution(mesh):
    in_specs = (
        P(None, "height", "cols", None),
        P(None, "height", "cols", None),
        P(None, "height", "cols"),
        P("height", "cols"),
        P("height", "cols"),
        P("height", "cols"),
        P("height", "cols", None),
        P("height", "cols", None),
        P("height", "cols", None),
    )
    out_specs = (
        P(None, "height", "cols", None),
        P(None, "height", "cols", None),
        P("height", "cols", None),
        P("height", "cols", None),
    )
    return jax.shard_map(
        on_device, mesh=mesh, in_specs=in_specs, out_specs=out_specs, check_vma=False
    )
```

profile of v0, /device:TPU:1, one launch (start us, length us, event | category | flops | bytes accessed | tf_op | source)
XLA Modules:
  0.0 536.4 jit_solution(15262174629706411374)
XLA Ops:
  1.5 16.0 %collective-permute-start.1 = (f32[6,1,8,128]{3,0,2,1:T(8,128)S(1)}, f32[6,1,8,128]{3,0,2,1:T(8,128)S(1)}, u32[]{:S(2)}, u32[]{:S(2)}) collective-permute-start(f32[6,1,8,128]{3,0,2,1:T(8,128)S(1)} %get-tuple-element.370), channel_id=1, source_target_pairs={{8,0},{16,8},{24,16},{32,24},{40,32},{48,40},{56,48},{64,56},{72,6... | collective-permute-start | bytes 73736 | tf_op jit(solution)/shard_map/ppermute | solution.py:26
  17.5 1.9 collective-permute-start
  19.4 1.2 collective-permute-done
  20.6 1.3 collective-permute-start.3
  21.9 4.0 collective-permute-start.2
  27.6 39.1 %while.22 = (s32[]{:T(128)}, f32[2,3,8,128]{3,2,0,1:T(8,128)S(1)}, s32[2]{0:T(128)S(1)}, f32[6,4,10,128]{3,0,2,1:T(8,128)S(1)}, s32[9,2,8]{2,1,0:T(2,128)S(1)}, ...) while((s32[]{:T(128)}, f32[2,3,8,128]{3,2,0,1:T(8,128)S(1)}, ...), condition=%wide.region_20.21_spmd.clone, body=%wide.region_0.20_spmd.sunk.clone.sunk | while | flops 94617760 | bytes 10712344 | solution.py:69
  31.6 1.1 fusion.516
  32.8 1.1 fusion.517
  34.5 1.1 fusion.519
  36.2 1.1 fusion.521
  37.9 1.1 fusion.523
  39.6 1.1 fusion.525
  41.3 1.1 fusion.527
  43.0 1.1 fusion.529
  44.7 1.1 fusion.531
  51.1 1.1 fusion.516
  52.2 1.1 fusion.517
  53.9 1.1 fusion.519
  55.7 1.1 fusion.521
  57.4 1.1 fusion.523
  59.0 1.1 fusion.525
  60.7 1.1 fusion.527
  62.4 1.1 fusion.529
  64.2 1.1 fusion.531
  67.4 3.2 collective-permute-start.5
  70.6 3.9 collective-permute-start.4
  75.5 1.3 collective-permute-start.7
  76.8 4.5 collective-permute-start.6
  82.5 39.1 %while.23 = (s32[]{:T(128)}, f32[2,3,8,128]{3,2,0,1:T(8,128)S(1)}, s32[2]{0:T(128)S(1)}, f32[6,4,10,128]{3,0,2,1:T(8,128)S(1)}, s32[9,2,8]{2,1,0:T(2,128)S(1)}, ...) while((s32[]{:T(128)}, f32[2,3,8,128]{3,2,0,1:T(8,128)S(1)}, ...), condition=%wide.region_41.42_spmd.clone, body=%wide.region_21.41_spmd.sunk.clone.sunk | while | flops 94617760 | bytes 10712344 | solution.py:69
  86.6 1.1 fusion.553
  87.7 1.1 fusion.554
  89.4 1.1 fusion.556
  91.1 1.1 fusion.558
  92.9 1.1 fusion.560
  94.5 1.1 fusion.562
  96.2 1.1 fusion.564
  97.9 1.1 fusion.566
  99.7 1.1 fusion.568
  106.0 1.1 fusion.553
  107.2 1.1 fusion.554
  108.9 1.1 fusion.556
  110.6 1.1 fusion.558
  112.3 1.1 fusion.560
  114.0 1.1 fusion.562
  115.7 1.1 fusion.564
  117.4 1.1 fusion.566
  119.1 1.1 fusion.568
  123.5 0.9 copy-done
  124.5 1.9 collective-permute-start.9
  126.4 4.8 collective-permute-start.10
  131.4 2.4 collective-permute-start.8
  133.9 1.3 collective-permute-start.11
  135.2 4.5 collective-permute-start.12
  140.8 0.8 multiply_reduce_fusion.20
  141.7 134.1 %all-reduce.2 = (f32[]{:T(128)}, f32[]{:T(128)}) all-reduce(f32[]{:T(128)} %get-tuple-element.267, f32[]{:T(128)} %get-tuple-element.266), channel_id=1, replica_groups=mesh['height'=128,'cols'=8] {'height','cols'}, use_global_device_ids=true, to_apply=%region_44.45 | all-reduce | flops 2 | bytes 16 | tf_op jit(solution)/shard_map/psum | solution.py:90
  277.8 117.3 %psum.30 = f32[]{:T(128)} all-reduce(f32[]{:T(128)} %get-tuple-element.292), channel_id=1, replica_groups=mesh['height'=128,'cols'=8] {'height','cols'}, use_global_device_ids=true, to_apply=%region_48.49 | all-reduce | flops 1 | bytes 8 | tf_op jit(solution)/shard_map/psum | solution.py:90
  396.5 2.6 collective-permute-start.13
  399.1 3.0 collective-permute-start.14
  402.8 1.2 collective-permute-done.14
  404.1 1.3 collective-permute-start.15
  405.4 4.0 collective-permute-start.16
  410.5 0.8 multiply_reduce_fusion.18
  411.3 123.0 %psum.31 = f32[]{:T(128)} all-reduce(f32[]{:T(128)} %get-tuple-element.290), channel_id=1, replica_groups=mesh['height'=128,'cols'=8] {'height','cols'}, use_global_device_ids=true, to_apply=%region_50.51 | all-reduce | flops 1 | bytes 8 | tf_op jit(solution)/shard_map/psum | solution.py:90
  535.5 0.9 multiply_subtract_fusion
  (145 shorter events, 34.6 us)
Async XLA Ops:
  0.6 0.8 copy-start.11
  1.5 18.0 %collective-permute-start.1 = (f32[6,1,8,128]{3,0,2,1:T(8,128)S(1)}, f32[6,1,8,128]{3,0,2,1:T(8,128)S(1)}, u32[]{:S(2)}, u32[]{:S(2)}) collective-permute-start(f32[6,1,8,128]{3,0,2,1:T(8,128)S(1)} %get-tuple-element.370), channel_id=1, source_target_pairs={{8,0},{16,8},{24,16},{32,24},{40,32},{48,40},{56,48},{64,56},{72,6... | collective-permute-start | bytes 73736 | tf_op jit(solution)/shard_map/ppermute | solution.py:26
  17.5 3.1 collective-permute-start
  20.6 5.3 copy-start.12
  20.6 5.3 copy-start.13
  20.6 5.4 %collective-permute-start.3 = (f32[6,4,1,128]{3,0,2,1:T(8,128)S(1)}, f32[6,4,1,128]{3,0,2,1:T(8,128)S(1)}, u32[]{:S(2)}, u32[]{:S(2)}) collective-permute-start(f32[6,4,1,128]{3,0,2,1:T(8,128)S(1)} %get-tuple-element.366), channel_id=1, source_target_pairs={{1,0},{2,1},{3,2},{4,3},{5,4},{6,5},{7,6},{9,8},{10,9},{11,10},{12... | collective-permute-start | bytes 36872 | tf_op jit(solution)/shard_map/ppermute | solution.py:26
  21.9 4.8 collective-permute-start.2
  26.8 0.7 copy-start.2
  26.8 0.7 copy-start.3
  26.8 0.7 copy-start.4
  26.8 0.7 copy-start.5
  26.9 0.7 copy-start.6
  26.9 0.7 copy-start.7
  26.9 0.7 copy-start.8
  26.9 0.7 copy-start.9
  27.6 39.1 %copy-start.10 = (f32[3,2,8,128]{3,2,1,0:T(8,128)S(1)}, f32[3,2,8,128]{3,2,1,0:T(8,128)}, u32[]{:S(2)}) copy-start(f32[3,2,8,128]{3,2,1,0:T(8,128)} %param.33) | copy-start | bytes 73732
  66.6 0.7 copy-start.14
  67.4 7.3 %collective-permute-start.5 = (f32[6,1,8,128]{3,2,1,0:T(8,128)S(1)}, f32[6,1,8,128]{3,2,1,0:T(8,128)S(1)}, u32[]{:S(2)}, u32[]{:S(2)}) collective-permute-start(f32[6,1,8,128]{3,2,1,0:T(8,128)S(1)} %get-tuple-element.374), channel_id=1, source_target_pairs={{8,0},{16,8},{24,16},{32,24},{40,32},{48,40},{56,48},{64,56},{72,6... | collective-permute-start | bytes 73736 | tf_op jit(solution)/shard_map/ppermute | solution.py:26
  70.6 4.8 collective-permute-start.4
  75.5 6.9 %collective-permute-start.7 = (f32[6,4,1,128]{3,2,1,0:T(1,128)S(1)}, f32[6,4,1,128]{3,2,1,0:T(1,128)S(1)}, u32[]{:S(2)}, u32[]{:S(2)}) collective-permute-start(f32[6,4,1,128]{3,2,1,0:T(1,128)S(1)} %get-tuple-element.368), channel_id=1, source_target_pairs={{1,0},{2,1},{3,2},{4,3},{5,4},{6,5},{7,6},{9,8},{10,9},{11,10},{12... | collective-permute-start | bytes 36872 | tf_op jit(solution)/shard_map/ppermute | solution.py:26
  76.8 5.6 %collective-permute-start.6 = (f32[6,4,1,128]{3,2,1,0:T(1,128)S(1)}, f32[6,4,1,128]{3,2,1,0:T(1,128)S(1)}, u32[]{:S(2)}, u32[]{:S(2)}) collective-permute-start(f32[6,4,1,128]{3,2,1,0:T(1,128)S(1)} %get-tuple-element.367), channel_id=1, source_target_pairs={{0,1},{1,2},{2,3},{3,4},{4,5},{5,6},{6,7},{8,9},{9,10},{10,11},{11... | collective-permute-start | bytes 36872 | tf_op jit(solution)/shard_map/ppermute | solution.py:23
  81.6 0.7 copy-start.17
  121.7 0.7 copy-start.16
  123.4 1.0 copy-start
  123.4 1.0 copy-start.1
  124.5 9.3 %collective-permute-start.9 = (f32[1,64,512]{2,1,0:T(8,128)S(1)}, f32[1,64,512]{2,1,0:T(8,128)S(1)}, u32[]{:S(2)}, u32[]{:S(2)}) collective-permute-start(f32[1,64,512]{2,1,0:T(8,128)S(1)} %get-tuple-element.364), channel_id=1, source_target_pairs={{8,0},{16,8},{24,16},{32,24},{40,32},{48,40},{56,48},{64,56},{72,6... | collective-permute-start | bytes 393224 | tf_op jit(solution)/shard_map/ppermute | solution.py:26
  126.4 7.4 %collective-permute-start.10 = (f32[1,64,512]{2,1,0:T(8,128)S(1)}, f32[1,64,512]{2,1,0:T(8,128)S(1)}, u32[]{:S(2)}, u32[]{:S(2)}) collective-permute-start(f32[1,64,512]{2,1,0:T(8,128)S(1)} %get-tuple-element.363), channel_id=1, source_target_pairs={{0,8},{8,16},{16,24},{24,32},{32,40},{40,48},{48,56},{56,64},{64,7... | collective-permute-start | bytes 393224 | tf_op jit(solution)/shard_map/ppermute | solution.py:23
  131.4 270.7 %collective-permute-start.8 = (f32[6,8,128]{2,1,0:T(8,128)S(1)}, f32[6,8,128]{2,1,0:T(8,128)S(1)}, u32[]{:S(2)}, u32[]{:S(2)}) collective-permute-start(f32[6,8,128]{2,1,0:T(8,128)S(1)} %convolution_bitcast_fusion.19), channel_id=1, source_target_pairs={{0,8},{8,16},{16,24},{24,32},{32,40},{40,48},{48,56},{56,64},{64,7... | collective-permute-start | bytes 73736 | tf_op jit(solution)/shard_map/ppermute | solution.py:34
  133.9 5.9 %collective-permute-start.11 = (f32[4,1,512]{2,1,0:T(1,128)S(1)}, f32[4,1,512]{2,1,0:T(1,128)S(1)}, u32[]{:S(2)}, u32[]{:S(2)}) collective-permute-start(f32[4,1,512]{2,1,0:T(1,128)S(1)} %get-tuple-element.360), channel_id=1, source_target_pairs={{1,0},{2,1},{3,2},{4,3},{5,4},{6,5},{7,6},{9,8},{10,9},{11,10},{12... | collective-permute-start | bytes 24584 | tf_op jit(solution)/shard_map/ppermute | solution.py:26
  135.2 5.3 collective-permute-start.12
  396.5 6.3 %collective-permute-start.13 = (f32[1,64,512]{2,1,0:T(8,128)S(1)}, f32[1,64,512]{2,1,0:T(8,128)S(1)}, u32[]{:S(2)}, u32[]{:S(2)}) collective-permute-start(f32[1,64,512]{2,1,0:T(8,128)S(1)} %get-tuple-element.362), channel_id=1, source_target_pairs={{8,0},{16,8},{24,16},{32,24},{40,32},{48,40},{56,48},{64,56},{72,6... | collective-permute-start | bytes 393224 | tf_op jit(solution)/shard_map/ppermute | solution.py:26
  399.1 3.0 copy-start.15
  399.1 4.9 collective-permute-start.14
  404.1 5.9 %collective-permute-start.15 = (f32[4,1,512]{2,1,0:T(1,128)S(1)}, f32[4,1,512]{2,1,0:T(1,128)S(1)}, u32[]{:S(2)}, u32[]{:S(2)}) collective-permute-start(f32[4,1,512]{2,1,0:T(1,128)S(1)} %get-tuple-element.358), channel_id=1, source_target_pairs={{1,0},{2,1},{3,2},{4,3},{5,4},{6,5},{7,6},{9,8},{10,9},{11,10},{12... | collective-permute-start | bytes 24584 | tf_op jit(solution)/shard_map/ppermute | solution.py:26
  405.4 4.8 collective-permute-start.16
where the time goes:
time: 540 us; the launch traced here: 536 us
  blocking collectives  374 us (69%)
  matrix products  62.7 us (12%)
  starting transfers between devices  62 us (11%)
  loops' own time  13.5 us (2%)
  local copies, waits for them, and re-layouts  7.43 us (1%)
  other arithmetic  5.92 us (1%)
    psum x3, blocking collectives, global_dot(): return lax.psum(jnp.sum(left * right), ('height', 'cols'))  374 us
    dot_general x36, matrix products, row_forces(): cross = jnp.einsum('cip,ciq->ipq', places, other_places, precision=highest)  41 us
    ppermute x8, starting transfers between devices, padded_2(): lax.ppermute(lax.slice_in_dim(block, block.shape[dim] - width, None, axis...  30.7 us
    ppermute x8, starting transfers between devices, padded_2(): lax.ppermute(lax.slice_in_dim(block, 0, width, axis=dim), axis, backward)  28.9 us
    dot_general x36, matrix products, row_forces(): jnp.einsum('ipq,ciq->cip', weight, other_places - damping * other[3:6], p...  20.5 us
    another operation x2, loops' own time, tile_forces(): stacked = lax.map(one_row, jnp.arange(count, dtype=jnp.int32))  13.5 us
  transfers between devices with their start and end apart: 17, of which 7 were waited for; matrix products, arithmetic and copies ran while one was open for 1% of the time, Pallas kernels for 0%

commit v1 on v0

v1 whole, which is shorter than its diff:
```python
import functools

import jax
import jax.numpy as jnp
from jax import lax
from jax.experimental import pallas as pl
from jax.experimental.pallas import tpu as pltpu
from jax.sharding import PartitionSpec as P

MESH = pl.DeviceIdType.MESH
F32 = jnp.float32
BF16 = jnp.bfloat16

spring = 0.05
cutoff_sq = 1.44
damping = 0.5
step_dt = 0.05
gravity = 1.0
deposit_gain = 2.0

PAD = 16
NT_DIMS = (((1,), (1,)), ((), ()))
TN_DIMS = (((0,), (0,)), ((), ()))


def split3(value):
    high = value.astype(BF16).astype(F32)
    rest = value - high
    mid = rest.astype(BF16).astype(F32)
    return high, mid, (rest - mid).astype(BF16).astype(F32)


def kernel(
    depth_z,
    pos_ref,
    vel_ref,
    slots_ref,
    contacts_ref,
    exit_ref,
    inlet_ref,
    blocks_ref,
    gas_ref,
    diag_ref,
    pos_out,
    vel_out,
    press_out,
    resid_out,
    tiles_a,
    tiles_b,
    grams,
    pulls,
    owns,
    total,
    settled,
    gas,
    scale,
    zed,
    image,
    weighed,
    twice,
    per_tile,
    block_row,
    leaving,
    arrived,
    row_a,
    rows_a,
    row_b,
    rows_b,
    load_sem,
    send_a,
    recv_a,
    send_b,
    recv_b,
    send_gas,
    recv_gas,
    send_diag,
    recv_diag,
    send_blk,
    recv_blk,
    send_dep,
    recv_dep,
    send_mig,
    recv_mig,
    send_ra,
    recv_ra,
    send_rb,
    recv_rb,
):
    high = lax.axis_size("height")
    wide = lax.axis_size("cols")
    h = lax.axis_index("height")
    c = lax.axis_index("cols")
    up = lax.rem(h + 1, high)
    down = lax.rem(h + high - 1, high)
    right = lax.rem(c + 1, wide)
    left = lax.rem(c + wide - 1, wide)
    goes = (
        (up, c),
        (down, c),
        (h, right),
        (h, left),
        (up, right),
        (up, left),
        (down, right),
        (down, left),
    )
    core = lax.rem(h, 2)
    z = lax.rem(h // 2, depth_z)
    x = h // (2 * depth_z)
    plane = (high // depth_z) * wide
    place = (x * 2 + core) * wide + c

    def z_peer(k):
        return ((x * depth_z + lax.rem(z + k, depth_z)) * 2 + core, c)

    def plane_peer(k):
        there = lax.rem(place + k, plane)
        pair = there // wide
        return (
            ((pair // 2) * depth_z + z) * 2 + lax.rem(pair, 2),
            lax.rem(there, wide),
        )

    own_rows = gas_ref.shape[1]
    first, last = PAD, PAD + own_rows
    own_span = pl.ds(first, own_rows)
    load_gas = pltpu.make_async_copy(
        gas_ref, gas.at[pl.ds(2, 2), own_span], load_sem.at[0]
    )
    load_diag = pltpu.make_async_copy(
        diag_ref, scale.at[pl.ds(2, 2), own_span], load_sem.at[1]
    )
    load_gas.start()
    load_diag.start()

    barrier = pltpu.get_barrier_semaphore()
    for target in goes:
        pl.semaphore_signal(barrier, inc=1, device_id=target, device_id_type=MESH)

    def greet_z(k, carry):
        pl.semaphore_signal(barrier, inc=1, device_id=z_peer(k), device_id_type=MESH)
        return carry

    def greet_plane(k, carry):
        pl.semaphore_signal(
            barrier, inc=1, device_id=plane_peer(k), device_id_type=MESH
        )
        return carry

    lax.fori_loop(1, depth_z, greet_z, 0)
    lax.fori_loop(1, plane, greet_plane, 0)

    def send(source, dest, send_sem, recv_sem, k):
        copy = pltpu.make_async_remote_copy(
            src_ref=source,
            dst_ref=dest,
            send_sem=send_sem.at[k],
            recv_sem=recv_sem.at[k],
            device_id=goes[k],
            device_id_type=MESH,
        )
        copy.start()
        return copy

    def send_tiles(tiles, send_sem, recv_sem):
        pairs = (
            (tiles.at[2, pl.ds(1, 8)], tiles.at[0, pl.ds(1, 8)]),
            (tiles.at[1, pl.ds(1, 8)], tiles.at[3, pl.ds(1, 8)]),
            (tiles.at[pl.ds(1, 2), 8], tiles.at[pl.ds(1, 2), 0]),
            (tiles.at[pl.ds(1, 2), 1], tiles.at[pl.ds(1, 2), 9]),
            (tiles.at[2, 8], tiles.at[0, 0]),
            (tiles.at[2, 1], tiles.at[0, 9]),
            (tiles.at[1, 8], tiles.at[3, 0]),
            (tiles.at[1, 1], tiles.at[3, 9]),
        )
        return [
            send(source, dest, send_sem, recv_sem, k)
            for k, (source, dest) in enumerate(pairs)
        ]

    def send_planes(field, send_sem, recv_sem):
        top, bottom = pl.ds(last - 8, 8), pl.ds(first, 8)
        before, after = pl.ds(first - 8, 8), pl.ds(last, 8)
        mid = pl.ds(2, 2)
        pairs = (
            (field.at[mid, own_span], field.at[pl.ds(0, 2), own_span]),
            (field.at[mid, own_span], field.at[pl.ds(4, 2), own_span]),
            (field.at[mid, top], field.at[mid, before]),
            (field.at[mid, bottom], field.at[mid, after]),
            (field.at[3, top], field.at[1, before]),
            (field.at[3, bottom], field.at[1, after]),
            (field.at[2, top], field.at[4, before]),
            (field.at[2, bottom], field.at[4, after]),
        )
        return [
            send(source, dest, send_sem, recv_sem, k)
            for k, (source, dest) in enumerate(pairs)
        ]

    comp = lax.broadcasted_iota(jnp.int32, (8, 128), 0)
    lane = lax.broadcasted_iota(jnp.int32, (8, 128), 1)

    for row in range(2):
        for part, ref in enumerate((pos_ref, vel_ref)):
            for axis in range(3):
                value = ref[axis, row]
                for col in range(8):
                    tiles_a[row + 1, col + 1, pl.ds(3 * part + axis, 1), :] = value[
                        col : col + 1
                    ]
        for col in range(8):
            tiles_a[row + 1, col + 1, pl.ds(6, 2), :] = jnp.zeros((2, 128), F32)

    blocks_vec = jnp.full((8, 128), -1, jnp.int32)
    for tile in range(16):
        blocks_vec = jnp.where(
            (lane < 48) & (lax.rem(lane, 16) == tile),
            blocks_ref[tile // 8, tile % 8],
            blocks_vec,
        )
    block_row[8] = blocks_vec.astype(F32)

    span = (2.0 * spring / cutoff_sq) ** 0.5

    def features(tiles, row, col, edge):
        tile = tiles[row, col]
        if edge is not None:
            tile = jnp.where(edge, tile, 0.0)
        shift_x = (col - 4.5) if isinstance(col, int) else (col.astype(F32) - 4.5)
        shift_z = (row - 1.5) if isinstance(row, int) else (row.astype(F32) - 1.5)
        shift = jnp.where(comp == 0, shift_x, jnp.where(comp == 2, shift_z, 0.0))
        at = tile + shift
        speed = pltpu.roll(tile, 5, 0)
        moving = at - damping * speed
        unit = jnp.where(comp < 3, span * at, 0.0)
        half = -0.5 * jnp.sum(unit * unit, axis=0, keepdims=True)
        gram = jnp.where(comp == 3, half, jnp.where(comp == 4, 1.0, unit))
        g_high, g_mid, g_low = split3(gram)
        lanes = pl.ds(col * 128, 128)
        if not isinstance(col, int):
            lanes = pl.ds(pl.multiple_of(col * 128, 128), 128)
        grams[row, :, lanes] = jnp.concatenate(
            [g_high, g_mid, g_high, g_mid, g_low, g_high], axis=0
        ).astype(BF16)
        pull = jnp.where(comp < 3, moving, jnp.where(comp == 3, 1.0, 0.0))
        p_high, p_mid, p_low = split3(pull)
        pulls[row, :, lanes] = jnp.concatenate(
            [jnp.where(comp < 4, p_high, pltpu.roll(p_low, 4, 0)), p_mid], axis=0
        ).astype(BF16)
        return unit, half

    def own_features(tiles, row, col):
        unit, half = features(tiles, row + 1, col + 1, None)
        gram = jnp.where(comp == 4, half + spring, jnp.where(comp == 3, 1.0, unit))
        f_high, f_mid, f_low = split3(gram)
        block = jnp.concatenate([f_high, f_high, f_mid, f_mid, f_high, f_low], axis=0)
        owns[row * 8 + col] = jnp.transpose(
            jnp.concatenate([block, jnp.zeros((80, 128), F32)], axis=0)
        )[:, :48].astype(BF16)
        total[row * 8 + col] = jnp.zeros((16, 128), F32)

    def interact(row, col, other):
        lanes = pl.ds(pl.multiple_of(col * 128, 128), 384)
        score = jnp.dot(
            owns[row * 8 + col], grams[other, :, lanes], preferred_element_type=F32
        )
        weight = jnp.maximum(score, 0.0)
        w_high = weight.astype(BF16)
        w_low = (weight - w_high.astype(F32)).astype(BF16)
        pull = pulls[other, :, lanes]
        kept = []
        for step in range(3):
            flag = contacts_ref[(other - row) * 3 + step, row, col].astype(F32)
            kept.append(
                pull[:, step * 128 : (step + 1) * 128]
                * jnp.full((16, 128), flag, F32).astype(BF16)
            )
        pull = jnp.concatenate(kept, axis=1)
        return lax.dot_general(
            pull, w_high, NT_DIMS, preferred_element_type=F32
        ) + lax.dot_general(pull, w_low, NT_DIMS, preferred_element_type=F32)

    def gather(row, col, others):
        result = interact(row, col, others[0])
        for other in others[1:]:
            result = result + interact(row, col, other)
        total[row * 8 + col] = total[row * 8 + col] + result

    def near(tiles):
        def make(index, carry):
            own_features(tiles, 0, index)
            own_features(tiles, 1, index)
            return carry

        lax.fori_loop(0, 8, make, 0)

        def inner(col, carry):
            gather(0, col, (1, 2))
            gather(1, col, (1, 2))
            return carry

        lax.fori_loop(1, 7, inner, 0)

    has_up, has_down = h < high - 1, h > 0
    has_right, has_left = c < wide - 1, c > 0

    def far(tiles):
        def beside(row, carry):
            features(tiles, row, 0, has_left)
            features(tiles, row, 9, has_right)
            return carry

        lax.fori_loop(1, 3, beside, 0)
        features(tiles, 0, 0, has_left & has_down)
        features(tiles, 0, 9, has_right & has_down)
        features(tiles, 3, 0, has_left & has_up)
        features(tiles, 3, 9, has_right & has_up)

        def above(col, carry):
            features(tiles, 0, col, has_down)
            features(tiles, 3, col, has_up)
            return carry

        lax.fori_loop(1, 9, above, 0)

        def inner(col, carry):
            gather(0, col, (0,))
            gather(1, col, (3,))
            return carry

        lax.fori_loop(1, 7, inner, 0)

        def outer(side, carry):
            gather(0, side * 7, (0, 1, 2))
            gather(1, side * 7, (1, 2, 3))
            return carry

        lax.fori_loop(0, 2, outer, 0)

    def advanced(tiles, row, col):
        tile = tiles[row + 1, col + 1]
        sums = total[row * 8 + col]
        front = sums[0:8]
        pulled = front + pltpu.roll(front, 4, 0) + sums[8:16]
        weight = front[3:4]
        shift = jnp.where(
            comp == 0,
            col.astype(F32) - 3.5,
            jnp.where(comp == 2, row - 0.5, 0.0),
        )
        moving = tile + shift - damping * pltpu.roll(tile, 5, 0)
        force = pltpu.roll(moving * weight - pulled, 3, 0)
        speeds = tile + step_dt * force - jnp.where(comp == 5, step_dt * gravity, 0.0)
        places = tile + step_dt * pltpu.roll(speeds, 5, 0)
        return jnp.where(comp < 3, places, jnp.where(comp < 6, speeds, 0.0))

    load_gas.wait()
    load_diag.wait()
    near(tiles_a)

    pl.semaphore_wait(barrier, 8 + (depth_z - 1) + (plane - 1))

    halo_a = send_tiles(tiles_a, send_a, recv_a)
    halo_gas = send_planes(gas, send_gas, recv_gas)
    halo_blk = [
        send(block_row.at[8], block_row.at[k], send_blk, recv_blk, k) for k in range(8)
    ]
    for copy in halo_a:
        copy.wait_recv()
    far(tiles_a)

    def first_step(col, carry):
        tiles_b[1, col + 1] = advanced(tiles_a, 0, col)
        tiles_b[2, col + 1] = advanced(tiles_a, 1, col)
        return carry

    lax.fori_loop(0, 8, first_step, 0)
    halo_b = send_tiles(tiles_b, send_b, recv_b)
    halo_diag = send_planes(scale, send_diag, recv_diag)
    near(tiles_b)
    for copy in halo_b:
        copy.wait_recv()
    far(tiles_b)

    count_row = lax.broadcasted_iota(jnp.int32, (128, 128), 0)

    def second_step(col, carry):
        for row in range(2):
            tile = advanced(tiles_b, row, col)
            settled[row * 8 + col] = tile
            lift = deposit_gain * tile[5:6]
            l_high, l_mid, l_low = split3(lift)
            rows = jnp.where(
                comp == 0,
                l_high,
                jnp.where(comp == 1, l_mid, jnp.where(comp == 2, l_low, 0.0)),
            )
            slot = slots_ref[row, pl.ds(col, 1), :]
            table = jnp.where(count_row == slot, 1.0, 0.0).astype(BF16)
            placed = lax.dot_general(
                jnp.concatenate([rows, jnp.zeros((8, 128), F32)], axis=0).astype(BF16),
                table,
                NT_DIMS,
                preferred_element_type=F32,
            )
            per_tile[8, pl.ds(row * 8 + col, 1), :] = jnp.sum(
                placed[0:8], axis=0, keepdims=True
            )
        return carry

    lax.fori_loop(0, 8, second_step, 0)
    halo_dep = [
        send(per_tile.at[8], per_tile.at[k], send_dep, recv_dep, k) for k in range(8)
    ]

    rank = jnp.int32(0)
    picks = [[None] * 8 for _ in range(8)]
    stays = []
    for col in range(8):
        flag = exit_ref[1, col]
        for k in range(8):
            picks[k][col] = jnp.where(rank == k, flag, 0).astype(F32)
        stays.append((1 - flag).astype(F32))
        rank = rank + flag
    for k in range(8):
        value = picks[k][0] * settled[8]
        for col in range(1, 8):
            value = value + picks[k][col] * settled[8 + col]
        leaving[k] = value
    move = pltpu.make_async_remote_copy(
        src_ref=leaving,
        dst_ref=arrived,
        send_sem=send_mig.at[0],
        recv_sem=recv_mig.at[0],
        device_id=(up, c),
        device_id_type=MESH,
    )
    move.start()

    for copy in halo_gas:
        copy.wait_recv()
    for copy in halo_diag:
        copy.wait_recv()
    for copy in halo_gas:
        copy.wait_send()
    for copy in halo_diag:
        copy.wait_send()
    for copy in halo_blk:
        copy.wait_recv()

    def enter(source, place_p, place_r, from_p, from_r, rows, valid):
        parts = jnp.concatenate(
            list(split3(per_tile[source])) + [jnp.zeros((80, 128), F32)], axis=0
        ).astype(BF16)
        owners = block_row[source][0:1]
        base = lax.broadcasted_iota(jnp.int32, (rows, 128), 0)
        for quarter in range(4):
            number = ((base + (from_p * own_rows + from_r)) * 4 + quarter).astype(F32)
            table = jnp.where(number == owners, 1.0, 0.0).astype(BF16)
            lanes = slice(quarter * 128, (quarter + 1) * 128)
            r0 = gas[place_p, place_r : place_r + rows, lanes] - jnp.dot(
                table, parts, preferred_element_type=F32
            )
            m = 1.0 / (6.0 + scale[place_p, place_r : place_r + rows, lanes])
            if valid is not None:
                m = jnp.where(valid, m, 0.0)
            gas[place_p, place_r : place_r + rows, lanes] = r0
            scale[place_p, place_r : place_r + rows, lanes] = m
            zed[place_p, place_r : place_r + rows, lanes] = m * r0

    far_row = own_rows - 8
    enter(8, 2, first, 0, 0, own_rows, None)
    enter(8, 3, first, 1, 0, own_rows, None)
    for copy in halo_dep:
        copy.wait_recv()
    enter(0, 0, first, 0, 0, own_rows, has_down)
    enter(0, 1, first, 1, 0, own_rows, has_down)
    enter(1, 4, first, 0, 0, own_rows, has_up)
    enter(1, 5, first, 1, 0, own_rows, has_up)
    for p in range(2):
        enter(2, 2 + p, first - 8, p, far_row, 8, has_left)
        enter(3, 2 + p, last, p, 0, 8, has_right)
    enter(4, 1, first - 8, 1, far_row, 8, has_left & has_down)
    enter(5, 1, last, 1, 0, 8, has_right & has_down)
    enter(6, 4, first - 8, 0, far_row, 8, has_left & has_up)
    enter(7, 4, last, 0, 0, 8, has_right & has_up)

    lane_w = lax.broadcasted_iota(jnp.int32, (8, 512), 1)

    def beside_sum(field, p, row):
        here = field[p, row : row + 8, :]
        ahead = jnp.where(lane_w == 0, 0.0, pltpu.roll(here, 1, 1))
        behind = jnp.where(lane_w == 511, 0.0, pltpu.roll(here, 511, 1))
        result = field[p + 1, row : row + 8, :] + field[p - 1, row : row + 8, :]
        result = result + field[p, row + 1 : row + 9, :]
        result = result + field[p, row - 1 : row + 7, :]
        return result + ahead + behind

    zero = jnp.zeros((8, 512), F32)
    dots = [zero, zero, zero, zero]
    for p in (2, 3, 1, 4):
        inside = p in (2, 3)
        start, stop = (first - 8, last + 8) if inside else (first, last)
        for row in range(start, stop, 8):
            r0 = gas[p, row : row + 8, :]
            u = r0 - beside_sum(zed, p, row)
            w = scale[p, row : row + 8, :] * u
            weighed[p, row : row + 8, :] = w
            if inside and first <= row < last:
                image[p, row : row + 8, :] = u
                z0 = zed[p, row : row + 8, :]
                dots[0] = dots[0] + r0 * z0
                dots[1] = dots[1] + z0 * u
                dots[2] = dots[2] + u * w
    for p in (2, 3):
        for row in range(first, last, 8):
            t = image[p, row : row + 8, :] - beside_sum(weighed, p, row)
            twice[p - 2, row - first : row - first + 8, :] = t
            dots[3] = dots[3] + weighed[p, row : row + 8, :] * t

    lane_one = lax.broadcasted_iota(jnp.int32, (1, 128), 1)
    mine = jnp.zeros((1, 128), F32)
    for k, dot in enumerate(dots):
        mine = jnp.where(lane_one == k, jnp.sum(dot), mine)
    row_a[0] = mine

    def reduce_over(count, peer, source, slots, send_sem, recv_sem):
        def begin(k, carry):
            pltpu.make_async_remote_copy(
                src_ref=source.at[0],
                dst_ref=slots.at[k - 1],
                send_sem=send_sem.at[k - 1],
                recv_sem=recv_sem.at[k - 1],
                device_id=peer(k),
                device_id_type=MESH,
            ).start()
            return carry

        lax.fori_loop(1, count, begin, 0)

        def end(k, carry):
            pltpu.make_async_remote_copy(
                src_ref=source.at[0],
                dst_ref=slots.at[k - 1],
                send_sem=send_sem.at[k - 1],
                recv_sem=recv_sem.at[k - 1],
                device_id=peer(k),
                device_id_type=MESH,
            ).wait()
            return carry

        return end

    end_a = reduce_over(depth_z, z_peer, row_a, rows_a, send_ra, recv_ra)

    move.wait()
    targets = [inlet_ref[0, k] for k in range(8)]
    for col in range(8):
        value = jnp.where(targets[0] == col, 1.0, 0.0) * arrived[0]
        for k in range(1, 8):
            value = value + jnp.where(targets[k] == col, 1.0, 0.0) * arrived[k]
        settled[col] = value
        settled[8 + col] = settled[8 + col] * stays[col]
    for row in range(2):
        for part, ref in enumerate((pos_out, vel_out)):
            for axis in range(3):
                for col in range(8):
                    ref[axis, row, pl.ds(col, 1), :] = settled[
                        row * 8 + col, pl.ds(3 * part + axis, 1), :
                    ]

    lax.fori_loop(1, depth_z, end_a, 0)
    mine = mine + jnp.sum(rows_a[...], axis=0)
    row_b[0] = mine
    end_b = reduce_over(plane, plane_peer, row_b, rows_b, send_rb, recv_rb)
    lax.fori_loop(1, plane, end_b, 0)
    mine = mine + jnp.sum(rows_b[...], axis=0)

    rz, energy, cross, third = (
        jnp.sum(jnp.where(lane_one == k, mine, 0.0), axis=1, keepdims=True)
        for k in range(4)
    )
    alpha = rz / energy
    renewed = alpha * alpha * cross - rz
    grow = 1.0 + renewed / rz
    second = renewed / (
        grow * grow * energy - 2.0 * grow * alpha * cross + alpha * alpha * third
    )
    near_factor = jnp.broadcast_to(alpha + second * grow, (8, 128))[:, 0:1]
    far_factor = jnp.broadcast_to(second * alpha, (8, 128))[:, 0:1]
    for p in range(2):
        for row in range(0, own_rows, 8):
            rows = slice(first + row, first + row + 8)
            press_out[p, row : row + 8, :] = (
                near_factor * zed[p + 2, rows, :]
                - far_factor * weighed[p + 2, rows, :]
            )
            resid_out[p, row : row + 8, :] = (
                gas[p + 2, rows, :]
                - near_factor * image[p + 2, rows, :]
                + far_factor * twice[p, row : row + 8, :]
            )

    for copy in halo_a + halo_b + halo_blk + halo_dep:
        copy.wait_send()


def on_device(
    depth_z,
    positions,
    velocities,
    contacts,
    exit_flags,
    inlet_slots,
    cell_blocks,
    cell_slots,
    gas_source,
    diagonal,
):
    high = lax.axis_size("height")
    plane = (high // depth_z) * lax.axis_size("cols")
    vmem = pl.BlockSpec(memory_space=pltpu.VMEM)
    smem = pl.BlockSpec(memory_space=pltpu.SMEM)
    hbm = pl.BlockSpec(memory_space=pl.ANY)
    dma = pltpu.SemaphoreType.DMA
    own_rows = gas_source.shape[1]
    grid = (6, own_rows + 2 * PAD, gas_source.shape[2])
    return pl.pallas_call(
        functools.partial(kernel, depth_z),
        out_shape=(
            jax.ShapeDtypeStruct(positions.shape, F32),
            jax.ShapeDtypeStruct(velocities.shape, F32),
            jax.ShapeDtypeStruct(gas_source.shape, F32),
            jax.ShapeDtypeStruct(gas_source.shape, F32),
        ),
        in_specs=[vmem, vmem, vmem, smem, smem, smem, smem, hbm, hbm],
        out_specs=(vmem, vmem, vmem, vmem),
        scratch_shapes=[
            pltpu.VMEM((4, 10, 8, 128), F32),
            pltpu.VMEM((4, 10, 8, 128), F32),
            pltpu.VMEM((4, 48, 1280), BF16),
            pltpu.VMEM((4, 16, 1280), BF16),
            pltpu.VMEM((16, 128, 48), BF16),
            pltpu.VMEM((16, 16, 128), F32),
            pltpu.VMEM((16, 8, 128), F32),
            pltpu.VMEM(grid, F32),
            pltpu.VMEM(grid, F32),
            pltpu.VMEM(grid, F32),
            pltpu.VMEM(grid, F32),
            pltpu.VMEM(grid, F32),
            pltpu.VMEM(gas_source.shape, F32),
            pltpu.VMEM((9, 16, 128), F32),
            pltpu.VMEM((9, 8, 128), F32),
            pltpu.VMEM((8, 8, 128), F32),
            pltpu.VMEM((8, 8, 128), F32),
            pltpu.VMEM((1, 1, 128), F32),
            pltpu.VMEM((depth_z - 1, 1, 128), F32),
            pltpu.VMEM((1, 1, 128), F32),
            pltpu.VMEM((plane - 1, 1, 128), F32),
            dma((2,)),
            dma((8,)),
            dma((8,)),
            dma((8,)),
            dma((8,)),
            dma((8,)),
            dma((8,)),
            dma((8,)),
            dma((8,)),
            dma((8,)),
            dma((8,)),
            dma((8,)),
            dma((8,)),
            dma((1,)),
            dma((1,)),
            dma((depth_z - 1,)),
            dma((depth_z - 1,)),
            dma((plane - 1,)),
            dma((plane - 1,)),
        ],
        compiler_params=pltpu.CompilerParams(
            collective_id=0, has_side_effects=True
        ),
    )(
        positions,
        velocities,
        cell_slots,
        contacts,
        exit_flags,
        inlet_slots,
        cell_blocks,
        gas_source,
        diagonal,
    )


def solution(mesh, depth_z=16):
    in_specs = (
        P(None, "height", "cols", None),
        P(None, "height", "cols", None),
        P(None, "height", "cols"),
        P("height", "cols"),
        P("height", "cols"),
        P("height", "cols"),
        P("height", "cols", None),
        P("height", "cols", None),
        P("height", "cols", None),
    )
    out_specs = (
        P(None, "height", "cols", None),
        P(None, "height", "cols", None),
        P("height", "cols", None),
        P("height", "cols", None),
    )
    return jax.shard_map(
        functools.partial(on_device, depth_z),
        mesh=mesh,
        in_specs=in_specs,
        out_specs=out_specs,
        check_vma=False,
    )
```

time: 540 us -> 81.3 us (0.15)
  blocking collectives: 374 us -> 0 us
  Pallas kernels: 0 us -> 74.5 us
  matrix products: 62.7 us -> 0 us
  starting transfers between devices: 62 us -> 0 us
  loops' own time: 13.5 us -> 0 us
  other arithmetic: 5.92 us -> 0 us
    psum x3 -> x0, blocking collectives: 374 us -> none  [global_dot(): return lax.psum(jnp.sum(left * right), ('height', 'cols'))]
    pallas_call x0 -> x1, Pallas kernels: none -> 74.5 us  [on_device(): pl.pallas_call(functools.partial(kernel, depth_z), out_shape=(jax.ShapeDt...]
    dot_general x76 -> x0, matrix products: 62.7 us -> none  [the longest x36 41 us: row_forces(): cross = jnp.einsum('cip,ciq->ipq', places, other_places, precision=highest)]
    ppermute x17 -> x0, starting transfers between devices: 62 us -> none  [the longest x8 30.7 us: padded_2(): lax.ppermute(lax.slice_in_dim(block, block.shape[dim] - width, None, axis...]
    another operation x2 -> x0, loops' own time: 13.5 us -> none  [tile_forces(): stacked = lax.map(one_row, jnp.arange(count, dtype=jnp.int32))]
  transfers between devices with their start and end apart: 17 -> 0, of which waited for: 7 -> 0; matrix products, arithmetic and copies ran while one was open for 1% -> 0% of each run, Pallas kernels for 0% -> 0%
where the time goes in v1:
time: 81.3 us; the launch traced here: 80.9 us
  Pallas kernels  74.5 us (92%)
  local copies, waits for them, and re-layouts  5.76 us (7%)
    pallas_call x1, Pallas kernels, on_device(): pl.pallas_call(functools.partial(kernel, depth_z), out_shape=(jax.ShapeDt...  74.5 us
    unnamed x9, local copies, waits for them, and re-layouts  5.76 us

profile of v1, /device:TPU:1, one launch (start us, length us, event | category | flops | bytes accessed | tf_op | source)
XLA Modules:
  0.0 80.9 jit_solution(14285958153188303543)
XLA Ops:
  0.6 1.4 %copy.13.contacts_ref = s32[9,2,8]{2,1,0:T(2,128)} copy(s32[9,2,8]{0,2,1:T(8,128)} %param.11) | data formatting | bytes 1152 | tf_op args[2]
  2.0 74.5 %shard_map.120 = (f32[3,2,8,128]{3,2,1,0:T(8,128)}, f32[3,2,8,128]{3,2,1,0:T(8,128)}, f32[2,64,512]{2,1,0:T(8,128)}, f32[2,64,512]{2,1,0:T(8,128)}) custom-call(f32[3,2,8,128]{3,2,1,0:T(8,128)} %pos_ref.1, f32[3,2,8,128]{3,2,1,0:T(8,128)} %vel_ref.1, s32[2,8,128]{2,1,0:T(8,128)} %slots_ref.1, s32[9,2,8]{2,1,0:T(2,128)} %copy.13.contacts_ref, ...), custom_call_target="tpu_custom_call" | custom-call | tf_op jit(solution)/shard_map/pallas_call | solution.py:628
  76.5 0.0 copy-start.1
  76.5 1.4 %copy.18 = f32[3,2,8,128]{3,2,1,0:T(8,128)} copy(f32[3,2,8,128]{3,2,1,0:T(8,128)} %get-tuple-element.8) | data formatting | bytes 49152
  77.9 0.0 copy-done.1
  77.9 0.6 copy.19
  78.5 0.0 copy-start
  78.5 1.7 %copy.20 = f32[2,64,512]{2,1,0:T(8,128)} copy(f32[2,64,512]{2,1,0:T(8,128)} %get-tuple-element.10) | data formatting | bytes 524288
  80.2 0.0 copy-done
  80.2 0.7 copy.21
Async XLA Ops:
  76.5 1.4 %copy-start.1 = (f32[3,2,8,128]{3,2,1,0:T(8,128)S(1)}, f32[3,2,8,128]{3,2,1,0:T(8,128)}, u32[]{:S(2)}) copy-start(f32[3,2,8,128]{3,2,1,0:T(8,128)} %get-tuple-element.9) | copy-start | bytes 73732
  78.5 1.7 %copy-start = (f32[2,64,512]{2,1,0:T(8,128)S(1)}, f32[2,64,512]{2,1,0:T(8,128)}, u32[]{:S(2)}) copy-start(f32[2,64,512]{2,1,0:T(8,128)} %get-tuple-element.11) | copy-start | bytes 786436

commit v2 on v1

--- a/solution.py
+++ b/solution.py
@@ -43,8 +43,12 @@
     diag_ref,
     pos_out,
     vel_out,
-    press_out,
-    resid_out,
+    right_out,
+    image_out,
+    twice_out,
+    sums_out,
+    pos_buf,
+    vel_buf,
     tiles_a,
     tiles_b,
     grams,
@@ -67,6 +71,9 @@
     row_b,
     rows_b,
     load_sem,
+    store_sem,
+    known_z,
+    known_p,
     send_a,
     recv_a,
     send_b,
@@ -107,19 +114,64 @@
     core = lax.rem(h, 2)
     z = lax.rem(h // 2, depth_z)
     x = h // (2 * depth_z)
-    plane = (high // depth_z) * wide
-    place = (x * 2 + core) * wide + c
-
-    def z_peer(k):
-        return ((x * depth_z + lax.rem(z + k, depth_z)) * 2 + core, c)
-
-    def plane_peer(k):
-        there = lax.rem(place + k, plane)
-        pair = there // wide
-        return (
-            ((pair // 2) * depth_z + z) * 2 + lax.rem(pair, 2),
-            lax.rem(there, wide),
-        )
+    depth_x = high // (2 * depth_z)
+
+    def z_peer(step):
+        return (x * depth_z + lax.rem(z + step, depth_z)) * 2 + core
+
+    def x_peer(step):
+        return (lax.rem(x + step, depth_x) * depth_z + z) * 2 + core
+
+    def y_peer(step):
+        return lax.rem(c + step, wide)
+
+    def far_first(steps, count):
+        return sorted(steps, key=lambda step: -min(step, count - step))
+
+    line_z = [z_peer(step) if step else h for step in range(depth_z)]
+    line_x = [x_peer(step) if step else h for step in range(depth_x)]
+    line_y = [y_peer(step) if step else c for step in range(wide)]
+    other_core = 1 - 2 * core
+    peers_a = [
+        (line_z[step] + flip * other_core, c)
+        for step in far_first(range(depth_z), depth_z)
+        for flip in range(2)
+        if step or flip
+    ]
+    peers_b = [
+        (line_x[step_x], line_y[step_y])
+        for step_y in far_first(range(wide), wide)
+        for step_x in far_first(range(depth_x), depth_x)
+        if step_x or step_y
+    ]
+
+    def signal(sem, target):
+        pl.semaphore_signal(sem, inc=1, device_id=target, device_id_type=MESH)
+
+    chain_z, chain_p = [], []
+    reach = 1
+    while reach < depth_z // 2:
+        chain_z.append(((z_peer(reach), c), (z_peer(depth_z - reach), c)))
+        reach *= 2
+    chain_z.append(((h + other_core, c),))
+    reach = 1
+    while reach < wide // 2:
+        chain_p.append(((h, y_peer(reach)), (h, y_peer(wide - reach))))
+        reach *= 2
+    for _ in range(depth_x // 2):
+        chain_p.append(((x_peer(1), c), (x_peer(depth_x - 1), c)))
+    stage = [0]
+
+    def spread():
+        now = stage[0]
+        for chain, sem in ((chain_z, known_z), (chain_p, known_p)):
+            if 0 < now <= len(chain):
+                pl.semaphore_wait(sem.at[now - 1], len(chain[now - 1]))
+        for chain, sem in ((chain_z, known_z), (chain_p, known_p)):
+            if now < len(chain):
+                for target in chain[now]:
+                    signal(sem.at[now], target)
+        stage[0] = now + 1
 
     own_rows = gas_ref.shape[1]
     first, last = PAD, PAD + own_rows
@@ -134,21 +186,14 @@
     load_diag.start()
 
     barrier = pltpu.get_barrier_semaphore()
-    for target in goes:
-        pl.semaphore_signal(barrier, inc=1, device_id=target, device_id_type=MESH)
-
-    def greet_z(k, carry):
-        pl.semaphore_signal(barrier, inc=1, device_id=z_peer(k), device_id_type=MESH)
-        return carry
-
-    def greet_plane(k, carry):
-        pl.semaphore_signal(
-            barrier, inc=1, device_id=plane_peer(k), device_id_type=MESH
-        )
-        return carry
-
-    lax.fori_loop(1, depth_z, greet_z, 0)
-    lax.fori_loop(1, plane, greet_plane, 0)
+    greeted = goes + (
+        (z_peer(1), c),
+        (z_peer(depth_z - 1), c),
+        (x_peer(1), c),
+        (x_peer(depth_x - 1), c),
+    )
+    for target in greeted:
+        signal(barrier, target)
 
     def send(source, dest, send_sem, recv_sem, k):
         copy = pltpu.make_async_remote_copy(
@@ -243,9 +288,17 @@
             [g_high, g_mid, g_high, g_mid, g_low, g_high], axis=0
         ).astype(BF16)
         pull = jnp.where(comp < 3, moving, jnp.where(comp == 3, 1.0, 0.0))
-        p_high, p_mid, p_low = split3(pull)
+        pull = jnp.where(comp < 4, pull, pltpu.roll(pull, 4, 0))
+        products = [
+            pull * jnp.where(comp < 4, unit[0:1], unit[1:2]),
+            pull * jnp.where(comp < 4, unit[2:3], half),
+            jnp.where(comp < 4, pull, 0.0),
+        ]
+        parts = [split3(product) for product in products]
         pulls[row, :, lanes] = jnp.concatenate(
-            [jnp.where(comp < 4, p_high, pltpu.roll(p_low, 4, 0)), p_mid], axis=0
+            [part[level] for level in range(3) for part in parts]
+            + [jnp.zeros((8, 128), F32)],
+            axis=0,
         ).astype(BF16)
         return unit, half
 
@@ -257,34 +310,30 @@
         owns[row * 8 + col] = jnp.transpose(
             jnp.concatenate([block, jnp.zeros((80, 128), F32)], axis=0)
         )[:, :48].astype(BF16)
-        total[row * 8 + col] = jnp.zeros((16, 128), F32)
-
-    def interact(row, col, other):
-        lanes = pl.ds(pl.multiple_of(col * 128, 128), 384)
-        score = jnp.dot(
-            owns[row * 8 + col], grams[other, :, lanes], preferred_element_type=F32
+        total[row * 8 + col] = jnp.zeros((24, 128), F32)
+
+    def gather(row, col, pieces):
+        spans = []
+        for other, start, count in pieces:
+            begin = (col + start) * 128
+            if not isinstance(col, int):
+                begin = pl.multiple_of(begin, 128)
+            spans.append((other, pl.ds(begin, count * 128)))
+        gram = jnp.concatenate([grams[other, :, lanes] for other, lanes in spans], 1)
+        pull = jnp.concatenate([pulls[other, :, lanes] for other, lanes in spans], 1)
+        score = jnp.dot(owns[row * 8 + col], gram, preferred_element_type=F32)
+        kept = []
+        for other, start, count in pieces:
+            for step in range(start, start + count):
+                flag = contacts_ref[row, col, (other - row) * 3 + step].astype(F32)
+                here = score[:, len(kept) * 128 : (len(kept) + 1) * 128]
+                kept.append(jnp.where(here > 0.0, flag, 0.0).astype(BF16))
+        result = lax.dot_general(
+            pull, jnp.concatenate(kept, 1), NT_DIMS, preferred_element_type=F32
         )
-        weight = jnp.maximum(score, 0.0)
-        w_high = weight.astype(BF16)
-        w_low = (weight - w_high.astype(F32)).astype(BF16)
-        pull = pulls[other, :, lanes]
-        kept = []
-        for step in range(3):
-            flag = contacts_ref[(other - row) * 3 + step, row, col].astype(F32)
-            kept.append(
-                pull[:, step * 128 : (step + 1) * 128]
-                * jnp.full((16, 128), flag, F32).astype(BF16)
-            )
-        pull = jnp.concatenate(kept, axis=1)
-        return lax.dot_general(
-            pull, w_high, NT_DIMS, preferred_element_type=F32
-        ) + lax.dot_general(pull, w_low, NT_DIMS, preferred_element_type=F32)
-
-    def gather(row, col, others):
-        result = interact(row, col, others[0])
-        for other in others[1:]:
-            result = result + interact(row, col, other)
-        total[row * 8 + col] = total[row * 8 + col] + result
+        total[row * 8 + col] = total[row * 8 + col] + (
+            result[0:24] + result[24:48] + result[48:72]
+        )
 
     def near(tiles):
         def make(index, carry):
@@ -295,11 +344,14 @@
         lax.fori_loop(0, 8, make, 0)
 
         def inner(col, carry):
-            gather(0, col, (1, 2))
-            gather(1, col, (1, 2))
+            gather(0, col, ((1, 0, 3), (2, 0, 3)))
+            gather(1, col, ((1, 0, 3), (2, 0, 3)))
             return carry
 
         lax.fori_loop(1, 7, inner, 0)
+        for row in range(2):
+            gather(row, 0, ((1, 1, 2), (2, 1, 2)))
+            gather(row, 7, ((1, 0, 2), (2, 0, 2)))
 
     has_up, has_down = h < high - 1, h > 0
     has_right, has_left = c < wide - 1, c > 0
@@ -324,32 +376,34 @@
         lax.fori_loop(1, 9, above, 0)
 
         def inner(col, carry):
-            gather(0, col, (0,))
-            gather(1, col, (3,))
+            gather(0, col, ((0, 0, 3),))
+            gather(1, col, ((3, 0, 3),))
             return carry
 
         lax.fori_loop(1, 7, inner, 0)
-
-        def outer(side, carry):
-            gather(0, side * 7, (0, 1, 2))
-            gather(1, side * 7, (1, 2, 3))
-            return carry
-
-        lax.fori_loop(0, 2, outer, 0)
+        for row in range(2):
+            gather(row, 0, ((3 * row, 0, 3), (1, 0, 1), (2, 0, 1)))
+            gather(row, 7, ((3 * row, 0, 3), (1, 2, 1), (2, 2, 1)))
 
     def advanced(tiles, row, col):
         tile = tiles[row + 1, col + 1]
         sums = total[row * 8 + col]
-        front = sums[0:8]
-        pulled = front + pltpu.roll(front, 4, 0) + sums[8:16]
-        weight = front[3:4]
         shift = jnp.where(
             comp == 0,
             col.astype(F32) - 3.5,
             jnp.where(comp == 2, row - 0.5, 0.0),
         )
-        moving = tile + shift - damping * pltpu.roll(tile, 5, 0)
-        force = pltpu.roll(moving * weight - pulled, 3, 0)
+        at = tile + shift
+        moving = at - damping * pltpu.roll(tile, 5, 0)
+        unit = jnp.where(comp < 3, span * at, 0.0)
+        half = -0.5 * jnp.sum(unit * unit, axis=0, keepdims=True)
+        pulled = (
+            sums[0:8] * jnp.where(comp < 4, unit[0:1], unit[1:2])
+            + sums[8:16] * jnp.where(comp < 4, unit[2:3], 1.0)
+            + sums[16:24] * (half + spring)
+        )
+        pulled = pulled + pltpu.roll(pulled, 4, 0)
+        force = pltpu.roll(moving * pulled[3:4] - pulled, 3, 0)
         speeds = tile + step_dt * force - jnp.where(comp == 5, step_dt * gravity, 0.0)
         places = tile + step_dt * pltpu.roll(speeds, 5, 0)
         return jnp.where(comp < 3, places, jnp.where(comp < 6, speeds, 0.0))
@@ -358,16 +412,19 @@
     load_diag.wait()
     near(tiles_a)
 
-    pl.semaphore_wait(barrier, 8 + (depth_z - 1) + (plane - 1))
+    pl.semaphore_wait(barrier, len(greeted))
 
     halo_a = send_tiles(tiles_a, send_a, recv_a)
     halo_gas = send_planes(gas, send_gas, recv_gas)
     halo_blk = [
         send(block_row.at[8], block_row.at[k], send_blk, recv_blk, k) for k in range(8)
     ]
+    spread()
     for copy in halo_a:
         copy.wait_recv()
+    spread()
     far(tiles_a)
+    spread()
 
     def first_step(col, carry):
         tiles_b[1, col + 1] = advanced(tiles_a, 0, col)
@@ -378,9 +435,11 @@
     halo_b = send_tiles(tiles_b, send_b, recv_b)
     halo_diag = send_planes(scale, send_diag, recv_diag)
     near(tiles_b)
+    spread()
     for copy in halo_b:
         copy.wait_recv()
     far(tiles_b)
+    spread()
 
     count_row = lax.broadcasted_iota(jnp.int32, (128, 128), 0)
 
@@ -524,34 +583,34 @@
         mine = jnp.where(lane_one == k, jnp.sum(dot), mine)
     row_a[0] = mine
 
-    def reduce_over(count, peer, source, slots, send_sem, recv_sem):
-        def begin(k, carry):
-            pltpu.make_async_remote_copy(
-                src_ref=source.at[0],
-                dst_ref=slots.at[k - 1],
-                send_sem=send_sem.at[k - 1],
-                recv_sem=recv_sem.at[k - 1],
-                device_id=peer(k),
-                device_id_type=MESH,
-            ).start()
-            return carry
-
-        lax.fori_loop(1, count, begin, 0)
-
-        def end(k, carry):
-            pltpu.make_async_remote_copy(
-                src_ref=source.at[0],
-                dst_ref=slots.at[k - 1],
-                send_sem=send_sem.at[k - 1],
-                recv_sem=recv_sem.at[k - 1],
-                device_id=peer(k),
-                device_id_type=MESH,
-            ).wait()
-            return carry
-
-        return end
-
-    end_a = reduce_over(depth_z, z_peer, row_a, rows_a, send_ra, recv_ra)
+    def share(peers, source, slots, send_sem, recv_sem):
+        copies = []
+        for k, target in enumerate(peers):
+            copies.append(
+                pltpu.make_async_remote_copy(
+                    src_ref=source.at[0],
+                    dst_ref=slots.at[k],
+                    send_sem=send_sem.at[k],
+                    recv_sem=recv_sem.at[k],
+                    device_id=target,
+                    device_id_type=MESH,
+                )
+            )
+            copies[-1].start()
+        return copies
+
+    sums_a = share(peers_a, row_a, rows_a, send_ra, recv_ra)
+    stores = [
+        pltpu.make_async_copy(
+            gas.at[pl.ds(2, 2), own_span], right_out, store_sem.at[0]
+        ),
+        pltpu.make_async_copy(
+            image.at[pl.ds(2, 2), own_span], image_out, store_sem.at[1]
+        ),
+        pltpu.make_async_copy(twice, twice_out, store_sem.at[2]),
+    ]
+    for copy in stores:
+        copy.start()
 
     move.wait()
     targets = [inlet_ref[0, k] for k in range(8)]
@@ -562,22 +621,42 @@
         settled[col] = value
         settled[8 + col] = settled[8 + col] * stays[col]
     for row in range(2):
-        for part, ref in enumerate((pos_out, vel_out)):
+        for part, ref in enumerate((pos_buf, vel_buf)):
             for axis in range(3):
                 for col in range(8):
                     ref[axis, row, pl.ds(col, 1), :] = settled[
                         row * 8 + col, pl.ds(3 * part + axis, 1), :
                     ]
 
-    lax.fori_loop(1, depth_z, end_a, 0)
+    stores += [
+        pltpu.make_async_copy(pos_buf, pos_out, store_sem.at[3]),
+        pltpu.make_async_copy(vel_buf, vel_out, store_sem.at[4]),
+    ]
+    for copy in stores[3:]:
+        copy.start()
+    for copy in halo_a + halo_b + halo_blk + halo_dep:
+        copy.wait_send()
+
+    for copy in sums_a:
+        copy.wait_recv()
     mine = mine + jnp.sum(rows_a[...], axis=0)
     row_b[0] = mine
-    end_b = reduce_over(plane, plane_peer, row_b, rows_b, send_rb, recv_rb)
-    lax.fori_loop(1, plane, end_b, 0)
-    mine = mine + jnp.sum(rows_b[...], axis=0)
-
+    sums_b = share(peers_b, row_b, rows_b, send_rb, recv_rb)
+    for copy in sums_a:
+        copy.wait_send()
+    for copy in stores:
+        copy.wait()
+    for copy in sums_b:
+        copy.wait_recv()
+    sums_out[...] = mine + jnp.sum(rows_b[...], axis=0)
+    for copy in sums_b:
+        copy.wait_send()
+
+
+def finish(sums, right, image, twice, diag, pos, vel, pos_out, vel_out, press, resid):
+    lane = lax.broadcasted_iota(jnp.int32, (1, 128), 1)
     rz, energy, cross, third = (
-        jnp.sum(jnp.where(lane_one == k, mine, 0.0), axis=1, keepdims=True)
+        jnp.sum(jnp.where(lane == k, sums[...], 0.0), axis=1, keepdims=True)
         for k in range(4)
     )
     alpha = rz / energy
@@ -589,20 +668,14 @@
     near_factor = jnp.broadcast_to(alpha + second * grow, (8, 128))[:, 0:1]
     far_factor = jnp.broadcast_to(second * alpha, (8, 128))[:, 0:1]
     for p in range(2):
-        for row in range(0, own_rows, 8):
-            rows = slice(first + row, first + row + 8)
-            press_out[p, row : row + 8, :] = (
-                near_factor * zed[p + 2, rows, :]
-                - far_factor * weighed[p + 2, rows, :]
-            )
-            resid_out[p, row : row + 8, :] = (
-                gas[p + 2, rows, :]
-                - near_factor * image[p + 2, rows, :]
-                + far_factor * twice[p, row : row + 8, :]
-            )
-
-    for copy in halo_a + halo_b + halo_blk + halo_dep:
-        copy.wait_send()
+        for row in range(0, right.shape[1], 8):
+            rows = slice(row, row + 8)
+            r0, u = right[p, rows, :], image[p, rows, :]
+            m = 1.0 / (6.0 + diag[p, rows, :])
+            press[p, rows, :] = m * (near_factor * r0 - far_factor * u)
+            resid[p, rows, :] = r0 - near_factor * u + far_factor * twice[p, rows, :]
+    pos_out[...] = pos[...]
+    vel_out[...] = vel[...]
 
 
 def on_device(
@@ -618,30 +691,31 @@
     diagonal,
 ):
     high = lax.axis_size("height")
-    plane = (high // depth_z) * lax.axis_size("cols")
+    count_a = 2 * depth_z - 1
+    count_b = (high // (2 * depth_z)) * lax.axis_size("cols") - 1
     vmem = pl.BlockSpec(memory_space=pltpu.VMEM)
     smem = pl.BlockSpec(memory_space=pltpu.SMEM)
     hbm = pl.BlockSpec(memory_space=pl.ANY)
     dma = pltpu.SemaphoreType.DMA
     own_rows = gas_source.shape[1]
     grid = (6, own_rows + 2 * PAD, gas_source.shape[2])
-    return pl.pallas_call(
+    field = jax.ShapeDtypeStruct(gas_source.shape, F32)
+    state = jax.ShapeDtypeStruct(positions.shape, F32)
+    row = jax.ShapeDtypeStruct((1, 128), F32)
+    pos, vel, right, image, twice, sums = pl.pallas_call(
         functools.partial(kernel, depth_z),
-        out_shape=(
-            jax.ShapeDtypeStruct(positions.shape, F32),
-            jax.ShapeDtypeStruct(velocities.shape, F32),
-            jax.ShapeDtypeStruct(gas_source.shape, F32),
-            jax.ShapeDtypeStruct(gas_source.shape, F32),
-        ),
+        out_shape=(state, state, field, field, field, row),
         in_specs=[vmem, vmem, vmem, smem, smem, smem, smem, hbm, hbm],
-        out_specs=(vmem, vmem, vmem, vmem),
+        out_specs=(hbm, hbm, hbm, hbm, hbm, vmem),
         scratch_shapes=[
+            pltpu.VMEM(positions.shape, F32),
+            pltpu.VMEM(positions.shape, F32),
             pltpu.VMEM((4, 10, 8, 128), F32),
             pltpu.VMEM((4, 10, 8, 128), F32),
             pltpu.VMEM((4, 48, 1280), BF16),
-            pltpu.VMEM((4, 16, 1280), BF16),
+            pltpu.VMEM((4, 80, 1280), BF16),
             pltpu.VMEM((16, 128, 48), BF16),
-            pltpu.VMEM((16, 16, 128), F32),
+            pltpu.VMEM((16, 24, 128), F32),
             pltpu.VMEM((16, 8, 128), F32),
             pltpu.VMEM(grid, F32),
             pltpu.VMEM(grid, F32),
@@ -654,10 +728,13 @@
             pltpu.VMEM((8, 8, 128), F32),
             pltpu.VMEM((8, 8, 128), F32),
             pltpu.VMEM((1, 1, 128), F32),
-            pltpu.VMEM((depth_z - 1, 1, 128), F32),
+            pltpu.VMEM((count_a, 1, 128), F32),
             pltpu.VMEM((1, 1, 128), F32),
-            pltpu.VMEM((plane - 1, 1, 128), F32),
+            pltpu.VMEM((count_b, 1, 128), F32),
             dma((2,)),
+            dma((5,)),
+            pltpu.SemaphoreType.REGULAR((8,)),
+            pltpu.SemaphoreType.REGULAR((8,)),
             dma((8,)),
             dma((8,)),
             dma((8,)),
@@ -672,10 +749,10 @@
             dma((8,)),
             dma((1,)),
             dma((1,)),
-            dma((depth_z - 1,)),
-            dma((depth_z - 1,)),
-            dma((plane - 1,)),
-            dma((plane - 1,)),
+            dma((count_a,)),
+            dma((count_a,)),
+            dma((count_b,)),
+            dma((count_b,)),
         ],
         compiler_params=pltpu.CompilerParams(
             collective_id=0, has_side_effects=True
@@ -684,13 +761,19 @@
         positions,
         velocities,
         cell_slots,
-        contacts,
+        jnp.transpose(contacts, (1, 2, 0)),
         exit_flags,
         inlet_slots,
         cell_blocks,
         gas_source,
         diagonal,
     )
+    return pl.pallas_call(
+        finish,
+        out_shape=(state, state, field, field),
+        in_specs=[vmem] * 7,
+        out_specs=(vmem,) * 4,
+    )(sums, right, image, twice, diagonal, pos, vel)
 
 
 def solution(mesh, depth_z=16):

time: 81.3 us -> 67.2 us (0.83)
  Pallas kernels: 74.5 us -> 66.3 us
  local copies, waits for them, and re-layouts: 5.76 us -> 0 us
    pallas_call x1 -> x2, Pallas kernels: 74.5 us -> 66.3 us  [the longest x1 64.1 us: on_device(): pl.pallas_call(functools.partial(kernel, depth_z), out_shape=(state, stat...]
    unnamed x9 -> x0, local copies, waits for them, and re-layouts: 5.76 us -> none
where the time goes in v2:
time: 67.2 us; the launch traced here: 66.9 us
  Pallas kernels  66.3 us (99%)
    pallas_call x1, Pallas kernels, on_device(): pl.pallas_call(functools.partial(kernel, depth_z), out_shape=(state, stat...  64.1 us
    pallas_call x1, Pallas kernels, on_device(): pl.pallas_call(finish, out_shape=(state, state, field, field), in_specs=[...  2.18 us

profile of v2, /device:TPU:1, one launch (start us, length us, event | category | flops | bytes accessed | tf_op | source)
XLA Modules:
  0.0 66.9 jit_solution(9751427629045814395)
XLA Ops:
  0.6 64.1 %shard_map.120 = (f32[3,2,8,128]{3,2,1,0:T(8,128)}, f32[3,2,8,128]{3,2,1,0:T(8,128)}, f32[2,64,512]{2,1,0:T(8,128)}, f32[2,64,512]{2,1,0:T(8,128)}, f32[2,64,512]{2,1,0:T(8,128)}, /*index=5*/f32[1,128]{1,0:T(1,128)}) custom-call(f32[3,2,8,128]{3,2,1,0:T(8,128)} %pos_ref.1, f32[3,2,8,128]{3,2,1,0:T(8,128)} %vel_ref.1, s32[2,8,128]{2,1,0:T(8,128)} %slots_ref.1, ...), custom_call_target="tpu_custom_call" | custom-call | tf_op jit(solution)/shard_map/pallas_call | solution.py:705
  64.7 2.2 %shard_map.121 = (f32[3,2,8,128]{3,2,1,0:T(8,128)}, f32[3,2,8,128]{3,2,1,0:T(8,128)}, f32[2,64,512]{2,1,0:T(8,128)}, f32[2,64,512]{2,1,0:T(8,128)}) custom-call(f32[1,128]{1,0:T(1,128)} %get-tuple-element.10.sums, f32[2,64,512]{2,1,0:T(8,128)} %get-tuple-element.11.right, f32[2,64,512]{2,1,0:T(8,128)} %get-tuple-element.12.image, ...), custom_call_target="tpu_custom_call" | custom-call | tf_op jit(solution)/shard_map/pallas_call | solution.py:771

commit v3 on v2

--- a/solution.py
+++ b/solution.py
@@ -58,6 +58,7 @@
     settled,
     gas,
     scale,
+    recip,
     zed,
     image,
     weighed,
@@ -307,51 +308,85 @@
         gram = jnp.where(comp == 4, half + spring, jnp.where(comp == 3, 1.0, unit))
         f_high, f_mid, f_low = split3(gram)
         block = jnp.concatenate([f_high, f_high, f_mid, f_mid, f_high, f_low], axis=0)
-        owns[row * 8 + col] = jnp.transpose(
+        owns[col, pl.ds(row * 128, 128), :] = jnp.transpose(
             jnp.concatenate([block, jnp.zeros((80, 128), F32)], axis=0)
         )[:, :48].astype(BF16)
-        total[row * 8 + col] = jnp.zeros((24, 128), F32)
-
-    def gather(row, col, pieces):
-        spans = []
-        for other, start, count in pieces:
-            begin = (col + start) * 128
-            if not isinstance(col, int):
-                begin = pl.multiple_of(begin, 128)
-            spans.append((other, pl.ds(begin, count * 128)))
-        gram = jnp.concatenate([grams[other, :, lanes] for other, lanes in spans], 1)
-        pull = jnp.concatenate([pulls[other, :, lanes] for other, lanes in spans], 1)
-        score = jnp.dot(owns[row * 8 + col], gram, preferred_element_type=F32)
-        kept = []
-        for other, start, count in pieces:
-            for step in range(start, start + count):
-                flag = contacts_ref[row, col, (other - row) * 3 + step].astype(F32)
-                here = score[:, len(kept) * 128 : (len(kept) + 1) * 128]
-                kept.append(jnp.where(here > 0.0, flag, 0.0).astype(BF16))
-        result = lax.dot_general(
-            pull, jnp.concatenate(kept, 1), NT_DIMS, preferred_element_type=F32
-        )
-        total[row * 8 + col] = total[row * 8 + col] + (
-            result[0:24] + result[24:48] + result[48:72]
-        )
-
-    def near(tiles):
+
+    def gather(jobs):
+        steps = []
+        for rows, col, pieces, fresh in jobs:
+            blocks = [
+                (other, step)
+                for other, start, count in pieces
+                for step in range(start, start + count)
+            ]
+            for at in range(0, len(blocks), 6):
+                last = at + 6 >= len(blocks)
+                steps.append((rows, col, blocks[at : at + 6], at == 0, last, fresh))
+
+        def stack(table, col, group):
+            parts = []
+            for other, step in group:
+                begin = (col + step) * 128
+                if not isinstance(col, int):
+                    begin = pl.multiple_of(begin, 128)
+                parts.append(table[other, :, pl.ds(begin, 128)])
+            return jnp.concatenate(parts, 1)
+
+        def score(rows, col, group, *_):
+            mine = owns[col, rows[0] * 128 : (rows[-1] + 1) * 128, :]
+            return jnp.dot(mine, stack(grams, col, group), preferred_element_type=F32)
+
+        ready = [score(*step) for step in steps[:1]]
+        result = None
+        for n, (rows, col, group, begins, ends, fresh) in enumerate(steps):
+            if n + 1 < len(steps):
+                ready.append(score(*steps[n + 1]))
+            scores = ready.pop(0)
+            kept = []
+            for k, row in enumerate(rows):
+                parts = []
+                for m, (other, step) in enumerate(group):
+                    flag = contacts_ref[row, col, (other - row) * 3 + step].astype(F32)
+                    here = scores[k * 128 : (k + 1) * 128, m * 128 : (m + 1) * 128]
+                    parts.append(jnp.where(here > 0.0, flag, 0.0).astype(BF16))
+                kept.append(jnp.concatenate(parts, 1))
+            part = lax.dot_general(
+                jnp.concatenate(kept, 0),
+                stack(pulls, col, group),
+                NT_DIMS,
+                preferred_element_type=F32,
+            )
+            result = part if begins else result + part
+            if ends:
+                span_p = slice(rows[0] * 128, (rows[-1] + 1) * 128)
+                if not fresh:
+                    result = result + total[col, span_p, 0:80]
+                total[col, span_p, 0:80] = result
+
+    def own_tiles(tiles):
         def make(index, carry):
             own_features(tiles, 0, index)
             own_features(tiles, 1, index)
             return carry
 
-        lax.fori_loop(0, 8, make, 0)
-
-        def inner(col, carry):
-            gather(0, col, ((1, 0, 3), (2, 0, 3)))
-            gather(1, col, ((1, 0, 3), (2, 0, 3)))
+        lax.fori_loop(0, 8, make, 0, unroll=2)
+
+    def near():
+        both = (0, 1)
+        gather(
+            [
+                (both, 0, ((1, 1, 2), (2, 1, 2)), True),
+                (both, 7, ((1, 0, 2), (2, 0, 2)), True),
+            ]
+        )
+
+        def inner(index, carry):
+            cols = [index * 2 + 1 + k for k in range(2)]
+            gather([(both, col, ((1, 0, 3), (2, 0, 3)), True) for col in cols])
             return carry
 
-        lax.fori_loop(1, 7, inner, 0)
-        for row in range(2):
-            gather(row, 0, ((1, 1, 2), (2, 1, 2)))
-            gather(row, 7, ((1, 0, 2), (2, 0, 2)))
+        lax.fori_loop(0, 6 // 2, inner, 0)
 
     has_up, has_down = h < high - 1, h > 0
     has_right, has_left = c < wide - 1, c > 0
@@ -373,21 +408,27 @@
             features(tiles, 3, col, has_up)
             return carry
 
-        lax.fori_loop(1, 9, above, 0)
-
-        def inner(col, carry):
-            gather(0, col, ((0, 0, 3),))
-            gather(1, col, ((3, 0, 3),))
+        lax.fori_loop(1, 9, above, 0, unroll=2)
+
+        def inner(index, carry):
+            jobs = []
+            for k in range(2):
+                jobs.append(((0,), index * 2 + 1 + k, ((0, 0, 3),), False))
+                jobs.append(((1,), index * 2 + 1 + k, ((3, 0, 3),), False))
+            gather(jobs)
             return carry
 
-        lax.fori_loop(1, 7, inner, 0)
+        lax.fori_loop(0, 6 // 2, inner, 0)
+        jobs = []
         for row in range(2):
-            gather(row, 0, ((3 * row, 0, 3), (1, 0, 1), (2, 0, 1)))
-            gather(row, 7, ((3 * row, 0, 3), (1, 2, 1), (2, 2, 1)))
+            jobs.append(((row,), 0, ((3 * row, 0, 3), (1, 0, 1), (2, 0, 1)), False))
+            jobs.append(((row,), 7, ((3 * row, 0, 3), (1, 2, 1), (2, 2, 1)), False))
+        gather(jobs)
 
     def advanced(tiles, row, col):
         tile = tiles[row + 1, col + 1]
-        sums = total[row * 8 + col]
+        sums = jnp.transpose(total[col, pl.ds(row * 128, 128), :])
+        sums = sums[0:24] + sums[24:48] + sums[48:72]
         shift = jnp.where(
             comp == 0,
             col.astype(F32) - 3.5,
@@ -408,18 +449,18 @@
         places = tile + step_dt * pltpu.roll(speeds, 5, 0)
         return jnp.where(comp < 3, places, jnp.where(comp < 6, speeds, 0.0))
 
+    pl.semaphore_wait(barrier, len(greeted))
+
+    halo_a = send_tiles(tiles_a, send_a, recv_a)
     load_gas.wait()
     load_diag.wait()
-    near(tiles_a)
-
-    pl.semaphore_wait(barrier, len(greeted))
-
-    halo_a = send_tiles(tiles_a, send_a, recv_a)
     halo_gas = send_planes(gas, send_gas, recv_gas)
     halo_blk = [
         send(block_row.at[8], block_row.at[k], send_blk, recv_blk, k) for k in range(8)
     ]
     spread()
+    own_tiles(tiles_a)
+    near()
     for copy in halo_a:
         copy.wait_recv()
     spread()
@@ -431,11 +472,22 @@
         tiles_b[2, col + 1] = advanced(tiles_a, 1, col)
         return carry
 
-    lax.fori_loop(0, 8, first_step, 0)
+    lax.fori_loop(0, 8, first_step, 0, unroll=4)
     halo_b = send_tiles(tiles_b, send_b, recv_b)
     halo_diag = send_planes(scale, send_diag, recv_diag)
-    near(tiles_b)
+    own_tiles(tiles_b)
+    near()
     spread()
+
+    def invert(place_p, place_r, rows, valid):
+        for row in range(place_r, place_r + rows, 8):
+            m = 1.0 / (6.0 + scale[place_p, row : row + 8, :])
+            if valid is not None:
+                m = jnp.where(valid, m, 0.0)
+            recip[place_p, row : row + 8, :] = m
+
+    invert(2, first, own_rows, None)
+    invert(3, first, own_rows, None)
     for copy in halo_b:
         copy.wait_recv()
     far(tiles_b)
@@ -467,7 +519,7 @@
             )
         return carry
 
-    lax.fori_loop(0, 8, second_step, 0)
+    lax.fori_loop(0, 8, second_step, 0, unroll=4)
     halo_dep = [
         send(per_tile.at[8], per_tile.at[k], send_dep, recv_dep, k) for k in range(8)
     ]
@@ -502,12 +554,10 @@
         copy.wait_recv()
     for copy in halo_gas:
         copy.wait_send()
-    for copy in halo_diag:
-        copy.wait_send()
     for copy in halo_blk:
         copy.wait_recv()
 
-    def enter(source, place_p, place_r, from_p, from_r, rows, valid):
+    def enter(source, place_p, place_r, from_p, from_r, rows):
         parts = jnp.concatenate(
             list(split3(per_tile[source])) + [jnp.zeros((80, 128), F32)], axis=0
         ).astype(BF16)
@@ -520,29 +570,37 @@
             r0 = gas[place_p, place_r : place_r + rows, lanes] - jnp.dot(
                 table, parts, preferred_element_type=F32
             )
-            m = 1.0 / (6.0 + scale[place_p, place_r : place_r + rows, lanes])
-            if valid is not None:
-                m = jnp.where(valid, m, 0.0)
+            m = recip[place_p, place_r : place_r + rows, lanes]
             gas[place_p, place_r : place_r + rows, lanes] = r0
-            scale[place_p, place_r : place_r + rows, lanes] = m
             zed[place_p, place_r : place_r + rows, lanes] = m * r0
 
     far_row = own_rows - 8
-    enter(8, 2, first, 0, 0, own_rows, None)
-    enter(8, 3, first, 1, 0, own_rows, None)
+    enter(8, 2, first, 0, 0, own_rows)
+    enter(8, 3, first, 1, 0, own_rows)
+    invert(0, first, own_rows, has_down)
+    invert(1, first, own_rows, has_down)
+    invert(4, first, own_rows, has_up)
+    invert(5, first, own_rows, has_up)
+    for p in range(2):
+        invert(2 + p, first - 8, 8, has_left)
+        invert(2 + p, last, 8, has_right)
+    invert(1, first - 8, 8, has_left & has_down)
+    invert(1, last, 8, has_right & has_down)
+    invert(4, first - 8, 8, has_left & has_up)
+    invert(4, last, 8, has_right & has_up)
     for copy in halo_dep:
         copy.wait_recv()
-    enter(0, 0, first, 0, 0, own_rows, has_down)
-    enter(0, 1, first, 1, 0, own_rows, has_down)
-    enter(1, 4, first, 0, 0, own_rows, has_up)
-    enter(1, 5, first, 1, 0, own_rows, has_up)
+    enter(0, 0, first, 0, 0, own_rows)
+    enter(0, 1, first, 1, 0, own_rows)
+    enter(1, 4, first, 0, 0, own_rows)
+    enter(1, 5, first, 1, 0, own_rows)
     for p in range(2):
-        enter(2, 2 + p, first - 8, p, far_row, 8, has_left)
-        enter(3, 2 + p, last, p, 0, 8, has_right)
-    enter(4, 1, first - 8, 1, far_row, 8, has_left & has_down)
-    enter(5, 1, last, 1, 0, 8, has_right & has_down)
-    enter(6, 4, first - 8, 0, far_row, 8, has_left & has_up)
-    enter(7, 4, last, 0, 0, 8, has_right & has_up)
+        enter(2, 2 + p, first - 8, p, far_row, 8)
+        enter(3, 2 + p, last, p, 0, 8)
+    enter(4, 1, first - 8, 1, far_row, 8)
+    enter(5, 1, last, 1, 0, 8)
+    enter(6, 4, first - 8, 0, far_row, 8)
+    enter(7, 4, last, 0, 0, 8)
 
     lane_w = lax.broadcasted_iota(jnp.int32, (8, 512), 1)
 
@@ -563,7 +621,7 @@
         for row in range(start, stop, 8):
             r0 = gas[p, row : row + 8, :]
             u = r0 - beside_sum(zed, p, row)
-            w = scale[p, row : row + 8, :] * u
+            w = recip[p, row : row + 8, :] * u
             weighed[p, row : row + 8, :] = w
             if inside and first <= row < last:
                 image[p, row : row + 8, :] = u
@@ -580,7 +638,11 @@
     lane_one = lax.broadcasted_iota(jnp.int32, (1, 128), 1)
     mine = jnp.zeros((1, 128), F32)
     for k, dot in enumerate(dots):
-        mine = jnp.where(lane_one == k, jnp.sum(dot), mine)
+        fold = jnp.sum(dot, axis=0, keepdims=True)
+        fold = fold[:, 0:128] + fold[:, 128:256] + fold[:, 256:384] + fold[:, 384:512]
+        fold = fold + pltpu.roll(fold, 64, 1)
+        fold = fold + pltpu.roll(fold, 32, 1)
+        mine = jnp.where(lane_one // 32 == k, fold, mine)
     row_a[0] = mine
 
     def share(peers, source, slots, send_sem, recv_sem):
@@ -634,7 +696,7 @@
     ]
     for copy in stores[3:]:
         copy.start()
-    for copy in halo_a + halo_b + halo_blk + halo_dep:
+    for copy in halo_a + halo_b + halo_diag + halo_blk + halo_dep:
         copy.wait_send()
 
     for copy in sums_a:
@@ -656,7 +718,7 @@
 def finish(sums, right, image, twice, diag, pos, vel, pos_out, vel_out, press, resid):
     lane = lax.broadcasted_iota(jnp.int32, (1, 128), 1)
     rz, energy, cross, third = (
-        jnp.sum(jnp.where(lane == k, sums[...], 0.0), axis=1, keepdims=True)
+        jnp.sum(jnp.where(lane // 32 == k, sums[...], 0.0), axis=1, keepdims=True)
         for k in range(4)
     )
     alpha = rz / energy
@@ -667,15 +729,17 @@
     )
     near_factor = jnp.broadcast_to(alpha + second * grow, (8, 128))[:, 0:1]
     far_factor = jnp.broadcast_to(second * alpha, (8, 128))[:, 0:1]
-    for p in range(2):
-        for row in range(0, right.shape[1], 8):
-            rows = slice(row, row + 8)
-            r0, u = right[p, rows, :], image[p, rows, :]
-            m = 1.0 / (6.0 + diag[p, rows, :])
-            press[p, rows, :] = m * (near_factor * r0 - far_factor * u)
-            resid[p, rows, :] = r0 - near_factor * u + far_factor * twice[p, rows, :]
-    pos_out[...] = pos[...]
-    vel_out[...] = vel[...]
+    for row in range(0, right.shape[1], 8):
+        rows = slice(row, row + 8)
+        r0, u = right[0, rows, :], image[0, rows, :]
+        m = 1.0 / (6.0 + diag[0, rows, :])
+        press[0, rows, :] = m * (near_factor * r0 - far_factor * u)
+        resid[0, rows, :] = r0 - near_factor * u + far_factor * twice[0, rows, :]
+
+    @pl.when(pl.program_id(0) + pl.program_id(1) == 0)
+    def _():
+        pos_out[...] = pos[...]
+        vel_out[...] = vel[...]
 
 
 def on_device(
@@ -714,9 +778,10 @@
             pltpu.VMEM((4, 10, 8, 128), F32),
             pltpu.VMEM((4, 48, 1280), BF16),
             pltpu.VMEM((4, 80, 1280), BF16),
-            pltpu.VMEM((16, 128, 48), BF16),
-            pltpu.VMEM((16, 24, 128), F32),
+            pltpu.VMEM((8, 256, 48), BF16),
+            pltpu.VMEM((8, 256, 128), F32),
             pltpu.VMEM((16, 8, 128), F32),
+            pltpu.VMEM(grid, F32),
             pltpu.VMEM(grid, F32),
             pltpu.VMEM(grid, F32),
             pltpu.VMEM(grid, F32),
@@ -768,11 +833,18 @@
         gas_source,
         diagonal,
     )
+    whole = pl.BlockSpec(positions.shape, lambda p, q: (0, 0, 0, 0))
+    part = pl.BlockSpec(
+        (1, own_rows // 2, gas_source.shape[2]), lambda p, q: (p, q, 0)
+    )
     return pl.pallas_call(
         finish,
+        grid=(2, 2),
         out_shape=(state, state, field, field),
-        in_specs=[vmem] * 7,
-        out_specs=(vmem,) * 4,
+        in_specs=[pl.BlockSpec((1, 128), lambda p, q: (0, 0))]
+        + [part] * 4
+        + [whole] * 2,
+        out_specs=(whole, whole, part, part),
     )(sums, right, image, twice, diagonal, pos, vel)
 
 

time: 67.2 us -> 62.2 us (0.926)
  Pallas kernels: 66.3 us -> 61.2 us
    pallas_call x1, Pallas kernels: 64.1 us -> 57.7 us  [on_device(): pl.pallas_call(functools.partial(kernel, depth_z), out_shape=(state, stat...]
    pallas_call x1, Pallas kernels: 2.18 us -> 3.52 us  [on_device(): pl.pallas_call(finish, grid=(2, 2), out_shape=(state, state, field, field...]
where the time goes in v3:
time: 62.2 us; the launch traced here: 61.8 us
  Pallas kernels  61.2 us (98%)
  between operations  0.64 us (1%)
    pallas_call x1, Pallas kernels, on_device(): pl.pallas_call(functools.partial(kernel, depth_z), out_shape=(state, stat...  57.7 us
    pallas_call x1, Pallas kernels, on_device(): pl.pallas_call(finish, grid=(2, 2), out_shape=(state, state, field, field...  3.52 us

profile of v3, /device:TPU:1, one launch (start us, length us, event | category | flops | bytes accessed | tf_op | source)
XLA Modules:
  0.0 61.8 jit_solution(15520587006244795803)
XLA Ops:
  0.6 57.7 %shard_map.120 = (f32[3,2,8,128]{3,2,1,0:T(8,128)}, f32[3,2,8,128]{3,2,1,0:T(8,128)}, f32[2,64,512]{2,1,0:T(8,128)}, f32[2,64,512]{2,1,0:T(8,128)}, f32[2,64,512]{2,1,0:T(8,128)}, /*index=5*/f32[1,128]{1,0:T(1,128)}) custom-call(f32[3,2,8,128]{3,2,1,0:T(8,128)} %pos_ref.1, f32[3,2,8,128]{3,2,1,0:T(8,128)} %vel_ref.1, s32[2,8,128]{2,1,0:T(8,128)} %slots_ref.1, ...), custom_call_target="tpu_custom_call" | custom-call | tf_op jit(solution)/shard_map/pallas_call | solution.py:769
  58.3 3.5 %shard_map.121 = (f32[3,2,8,128]{3,2,1,0:T(8,128)}, f32[3,2,8,128]{3,2,1,0:T(8,128)}, f32[2,64,512]{2,1,0:T(8,128)}, f32[2,64,512]{2,1,0:T(8,128)}) custom-call(f32[1,128]{1,0:T(1,128)} %get-tuple-element.10.sums, f32[2,64,512]{2,1,0:T(8,128)} %get-tuple-element.11.right, f32[2,64,512]{2,1,0:T(8,128)} %get-tuple-element.12.image, ...), custom_call_target="tpu_custom_call" | custom-call | tf_op jit(solution)/shard_map/pallas_call | solution.py:840

commit v4 on v3

--- a/solution.py
+++ b/solution.py
@@ -221,7 +221,7 @@
         )
         return [
             send(source, dest, send_sem, recv_sem, k)
-            for k, (source, dest) in enumerate(pairs)
+            for k, (source, dest) in reversed(list(enumerate(pairs)))
         ]
 
     def send_planes(field, send_sem, recv_sem):
@@ -240,7 +240,7 @@
         )
         return [
             send(source, dest, send_sem, recv_sem, k)
-            for k, (source, dest) in enumerate(pairs)
+            for k, (source, dest) in reversed(list(enumerate(pairs)))
         ]
 
     comp = lax.broadcasted_iota(jnp.int32, (8, 128), 0)
@@ -450,6 +450,7 @@
         return jnp.where(comp < 3, places, jnp.where(comp < 6, speeds, 0.0))
 
     pl.semaphore_wait(barrier, len(greeted))
+    spread()
 
     halo_a = send_tiles(tiles_a, send_a, recv_a)
     load_gas.wait()
@@ -458,7 +459,6 @@
     halo_blk = [
         send(block_row.at[8], block_row.at[k], send_blk, recv_blk, k) for k in range(8)
     ]
-    spread()
     own_tiles(tiles_a)
     near()
     for copy in halo_a:
@@ -521,7 +521,8 @@
 
     lax.fori_loop(0, 8, second_step, 0, unroll=4)
     halo_dep = [
-        send(per_tile.at[8], per_tile.at[k], send_dep, recv_dep, k) for k in range(8)
+        send(per_tile.at[8], per_tile.at[k], send_dep, recv_dep, k)
+        for k in reversed(range(8))
     ]
 
     rank = jnp.int32(0)
@@ -729,17 +730,15 @@
     )
     near_factor = jnp.broadcast_to(alpha + second * grow, (8, 128))[:, 0:1]
     far_factor = jnp.broadcast_to(second * alpha, (8, 128))[:, 0:1]
-    for row in range(0, right.shape[1], 8):
-        rows = slice(row, row + 8)
-        r0, u = right[0, rows, :], image[0, rows, :]
-        m = 1.0 / (6.0 + diag[0, rows, :])
-        press[0, rows, :] = m * (near_factor * r0 - far_factor * u)
-        resid[0, rows, :] = r0 - near_factor * u + far_factor * twice[0, rows, :]
-
-    @pl.when(pl.program_id(0) + pl.program_id(1) == 0)
-    def _():
-        pos_out[...] = pos[...]
-        vel_out[...] = vel[...]
+    for p in range(2):
+        for row in range(0, right.shape[1], 8):
+            rows = slice(row, row + 8)
+            r0, u = right[p, rows, :], image[p, rows, :]
+            m = 1.0 / (6.0 + diag[p, rows, :])
+            press[p, rows, :] = m * (near_factor * r0 - far_factor * u)
+            resid[p, rows, :] = r0 - near_factor * u + far_factor * twice[p, rows, :]
+    pos_out[...] = pos[...]
+    vel_out[...] = vel[...]
 
 
 def on_device(
@@ -833,18 +832,11 @@
         gas_source,
         diagonal,
     )
-    whole = pl.BlockSpec(positions.shape, lambda p, q: (0, 0, 0, 0))
-    part = pl.BlockSpec(
-        (1, own_rows // 2, gas_source.shape[2]), lambda p, q: (p, q, 0)
-    )
     return pl.pallas_call(
         finish,
-        grid=(2, 2),
         out_shape=(state, state, field, field),
-        in_specs=[pl.BlockSpec((1, 128), lambda p, q: (0, 0))]
-        + [part] * 4
-        + [whole] * 2,
-        out_specs=(whole, whole, part, part),
+        in_specs=[vmem] * 7,
+        out_specs=(vmem,) * 4,
     )(sums, right, image, twice, diagonal, pos, vel)
 
 

time: 62.2 us -> 60.4 us (0.971)
  Pallas kernels: 61.2 us -> 59.6 us
    pallas_call x1, Pallas kernels: 3.52 us -> 2.19 us  [on_device(): pl.pallas_call(finish, out_shape=(state, state, field, field), in_specs=[...]
where the time goes in v4:
time: 60.4 us; the launch traced here: 60.2 us
  Pallas kernels  59.6 us (99%)
  between operations  0.64 us (1%)
    pallas_call x1, Pallas kernels, on_device(): pl.pallas_call(functools.partial(kernel, depth_z), out_shape=(state, stat...  57.4 us
    pallas_call x1, Pallas kernels, on_device(): pl.pallas_call(finish, out_shape=(state, state, field, field), in_specs=[...  2.19 us

profile of v4, /device:TPU:1, one launch (start us, length us, event | category | flops | bytes accessed | tf_op | source)
XLA Modules:
  0.0 60.2 jit_solution(13785152713947583914)
XLA Ops:
  0.6 57.4 %shard_map.120 = (f32[3,2,8,128]{3,2,1,0:T(8,128)}, f32[3,2,8,128]{3,2,1,0:T(8,128)}, f32[2,64,512]{2,1,0:T(8,128)}, f32[2,64,512]{2,1,0:T(8,128)}, f32[2,64,512]{2,1,0:T(8,128)}, /*index=5*/f32[1,128]{1,0:T(1,128)}) custom-call(f32[3,2,8,128]{3,2,1,0:T(8,128)} %pos_ref.1, f32[3,2,8,128]{3,2,1,0:T(8,128)} %vel_ref.1, s32[2,8,128]{2,1,0:T(8,128)} %slots_ref.1, ...), custom_call_target="tpu_custom_call" | custom-call | tf_op jit(solution)/shard_map/pallas_call | solution.py:768
  58.0 2.2 %shard_map.121 = (f32[3,2,8,128]{3,2,1,0:T(8,128)}, f32[3,2,8,128]{3,2,1,0:T(8,128)}, f32[2,64,512]{2,1,0:T(8,128)}, f32[2,64,512]{2,1,0:T(8,128)}) custom-call(f32[1,128]{1,0:T(1,128)} %get-tuple-element.10.sums, f32[2,64,512]{2,1,0:T(8,128)} %get-tuple-element.11.right, f32[2,64,512]{2,1,0:T(8,128)} %get-tuple-element.12.image, ...), custom_call_target="tpu_custom_call" | custom-call | tf_op jit(solution)/shard_map/pallas_call | solution.py:835

commit v5 on v4

--- a/solution.py
+++ b/solution.py
@@ -716,7 +716,48 @@
         copy.wait_send()
 
 
-def finish(sums, right, image, twice, diag, pos, vel, pos_out, vel_out, press, resid):
+def finish(
+    sums_in,
+    right_in,
+    image_in,
+    twice_in,
+    diag_in,
+    pos_in,
+    vel_in,
+    pos_out,
+    vel_out,
+    press_out,
+    resid_out,
+    sums,
+    right,
+    image,
+    twice,
+    diag,
+    state,
+    press,
+    resid,
+    sem,
+    load_sem,
+    store_sem,
+):
+    first = [
+        pltpu.make_async_copy(sums_in, sums, sem.at[0]),
+        pltpu.make_async_copy(pos_in, state.at[0], sem.at[1]),
+        pltpu.make_async_copy(vel_in, state.at[1], sem.at[2]),
+    ]
+    first[0].start()
+    loads = [
+        [
+            pltpu.make_async_copy(source.at[p], dest.at[p], load_sem.at[p, k])
+            for k, (source, dest) in enumerate(
+                ((right_in, right), (image_in, image), (twice_in, twice), (diag_in, diag))
+            )
+        ]
+        for p in range(2)
+    ]
+    for copy in loads[0] + loads[1] + first[1:]:
+        copy.start()
+    first[0].wait()
     lane = lax.broadcasted_iota(jnp.int32, (1, 128), 1)
     rz, energy, cross, third = (
         jnp.sum(jnp.where(lane // 32 == k, sums[...], 0.0), axis=1, keepdims=True)
@@ -730,15 +771,27 @@
     )
     near_factor = jnp.broadcast_to(alpha + second * grow, (8, 128))[:, 0:1]
     far_factor = jnp.broadcast_to(second * alpha, (8, 128))[:, 0:1]
+    stores = []
     for p in range(2):
+        for copy in loads[p]:
+            copy.wait()
         for row in range(0, right.shape[1], 8):
             rows = slice(row, row + 8)
             r0, u = right[p, rows, :], image[p, rows, :]
             m = 1.0 / (6.0 + diag[p, rows, :])
             press[p, rows, :] = m * (near_factor * r0 - far_factor * u)
             resid[p, rows, :] = r0 - near_factor * u + far_factor * twice[p, rows, :]
-    pos_out[...] = pos[...]
-    vel_out[...] = vel[...]
+        for k, (source, dest) in enumerate(((press, press_out), (resid, resid_out))):
+            stores.append(
+                pltpu.make_async_copy(source.at[p], dest.at[p], store_sem.at[p, k])
+            )
+            stores[-1].start()
+    for k, dest in enumerate((pos_out, vel_out)):
+        first[1 + k].wait()
+        stores.append(pltpu.make_async_copy(state.at[k], dest, store_sem.at[2, k]))
+        stores[-1].start()
+    for copy in stores:
+        copy.wait()
 
 
 def on_device(
@@ -835,8 +888,13 @@
     return pl.pallas_call(
         finish,
         out_shape=(state, state, field, field),
-        in_specs=[vmem] * 7,
-        out_specs=(vmem,) * 4,
+        in_specs=[hbm] * 7,
+        out_specs=(hbm,) * 4,
+        scratch_shapes=[pltpu.VMEM((1, 128), F32)]
+        + [pltpu.VMEM(gas_source.shape, F32)] * 4
+        + [pltpu.VMEM((2,) + positions.shape, F32)]
+        + [pltpu.VMEM(gas_source.shape, F32)] * 2
+        + [dma((3,)), dma((2, 4)), dma((3, 2))],
     )(sums, right, image, twice, diagonal, pos, vel)
 
 

time: 60.4 us -> 60.4 us (level)
  no operation moved by 1% of the time
where the time goes in v5:
time: 60.4 us; the launch traced here: 60.2 us
  Pallas kernels  59.6 us (99%)
  between operations  0.64 us (1%)
    pallas_call x1, Pallas kernels, on_device(): pl.pallas_call(functools.partial(kernel, depth_z), out_shape=(state, stat...  57.4 us
    pallas_call x1, Pallas kernels, on_device(): pl.pallas_call(finish, out_shape=(state, state, field, field), in_specs=[...  2.18 us

profile of v5, /device:TPU:1, one launch (start us, length us, event | category | flops | bytes accessed | tf_op | source)
XLA Modules:
  0.0 60.2 jit_solution(2827018185864590442)
XLA Ops:
  0.6 57.4 %shard_map.120 = (f32[3,2,8,128]{3,2,1,0:T(8,128)}, f32[3,2,8,128]{3,2,1,0:T(8,128)}, f32[2,64,512]{2,1,0:T(8,128)}, f32[2,64,512]{2,1,0:T(8,128)}, f32[2,64,512]{2,1,0:T(8,128)}, /*index=5*/f32[1,128]{1,0:T(1,128)}) custom-call(f32[3,2,8,128]{3,2,1,0:T(8,128)} %pos_ref.1, f32[3,2,8,128]{3,2,1,0:T(8,128)} %vel_ref.1, s32[2,8,128]{2,1,0:T(8,128)} %slots_ref.1, ...), custom_call_target="tpu_custom_call" | custom-call | tf_op jit(solution)/shard_map/pallas_call | solution.py:821
  58.0 2.2 %shard_map.121 = (f32[3,2,8,128]{3,2,1,0:T(8,128)}, f32[3,2,8,128]{3,2,1,0:T(8,128)}, f32[2,64,512]{2,1,0:T(8,128)}, f32[2,64,512]{2,1,0:T(8,128)}) custom-call(f32[1,128]{1,0:T(1,128)} %get-tuple-element.10.sums_in, f32[2,64,512]{2,1,0:T(8,128)} %get-tuple-element.11.right_in, f32[2,64,512]{2,1,0:T(8,128)} %get-tuple-element.12.image_in, ...), custom_call_target="tpu_custom_call" | custom-call | tf_op jit(solution)/shard_map/pallas_call | solution.py:888
